TPU v7x, 32 devices: a whole 2x2x4 slice. The times are simulated.
32 devices in a mesh: section: 2 (over y), dp: 16 (over z, x, core).
Axes of the slice: x: 2, y: 2, z: 4, core: 2. Of those that a mesh axis runs over, the one named last changes fastest.
Arguments:
- queries: bfloat16 [2, 16, 256, 2560], P('section', 'dp'), may hold values from -32 to 32
- keys: bfloat16 [16, 256, 512], P('dp', 'section'), may hold values from -12 to 12
- values: bfloat16 [16, 256, 512], P('dp', 'section'), may hold values from -6 to 6
- query_gain: float32 [2, 2560], P('section'), may hold values from 0.5 to 1.5
- key_channel_scale: float32 [2, 512], P('section'), may hold values from 0.5 to 1.5
- out_grad: bfloat16 [2, 16, 256, 2560], P('section', 'dp'), may hold values from -110 to 110
- doc_start: int32 [16], P('dp'), may hold values from 1 to 255
Outputs:
- query_grad: bfloat16 [2, 16, 256, 2560], P('section', 'dp')
- key_grad: bfloat16 [16, 256, 512], P('dp', 'section')
- value_grad: bfloat16 [16, 256, 512], P('dp', 'section')
- query_gain_grad: float32 [2, 2560], P('section')
- key_gain_grad: float32 [2, 512], P('section')
All inputs are finite; a program needn't handle non-finite values.
Results may differ from a plain program's by a relative error of at most 0.012.
The roundings to bfloat16 on the way count: a program that leaves them out, or rounds other values in their place, can miss the bound.
Values may be sent and summed in bfloat16 or wider, within the bound.
A program may use at most 64 MiB of HBM per device.

v0:
```python
import functools
import math

import jax
import jax.numpy as jnp
from jax import lax
from jax.experimental import pallas as pl
from jax.experimental.pallas import tpu as pltpu
from jax.sharding import PartitionSpec as P

HEAD = 128
LAG = 2
MESH = pl.DeviceIdType.MESH
BF = jnp.bfloat16
F32 = jnp.float32
NT = (((1,), (1,)), ((), ()))


def radices(n):
    out = []
    for r in (4, 3, 2, 5, 7):
        while n % r == 0:
            out.append(r)
            n //= r
    if n > 1:
        out.append(n)
    return out


def kernel(
    sections, replicas, stages,
    doc_hbm, q_hbm, k_hbm, v_hbm, qs_hbm, ks_hbm, do_hbm,
    dq_ref, kg_ref, vg_ref, qgain_ref, kgain_ref,
    doc_ref, qs_ref, ks_ref, q_vm, do_vm, k_vm, v_vm, bias, grad, gsend, grecv, *rest,
):
    n_st = len(stages)
    slots = rest[:n_st]
    (small_sem, q_sem, do_sem, kl_sem, vl_sem, k_ss, k_rs, v_ss, v_rs, g_ss, g_rs) = rest[n_st:n_st + 11]
    st_ss = rest[n_st + 11:2 * n_st + 11]
    st_rs = rest[2 * n_st + 11:]
    groups, length, width = q_vm.shape
    per = width // HEAD
    rows = k_hbm.shape[1]
    half = length // 2
    scale = HEAD ** -0.5
    to_exp2 = scale * math.log2(math.e)
    sec = lax.axis_index("section")
    dp = lax.axis_index("dp")

    def sec_peer(off):
        return lax.rem(sec + off, sections)

    strides = []
    stride = 1
    for r in stages:
        strides.append(stride)
        stride *= r

    def member(s):
        return lax.rem(dp // strides[s], stages[s])

    def st_peer(s, off):
        mine = member(s)
        other = lax.rem(mine + off, stages[s])
        return dp + (other - mine) * strides[s]

    barrier = pltpu.get_barrier_semaphore()
    count = 0
    for off in range(1, sections):
        pl.semaphore_signal(barrier, inc=1, device_id={"section": sec_peer(off)}, device_id_type=MESH)
        count += 1
    for s in range(n_st):
        for off in range(1, stages[s]):
            pl.semaphore_signal(barrier, inc=1, device_id={"dp": st_peer(s, off)}, device_id_type=MESH)
            count += 1

    my_rows = pl.ds(pl.multiple_of(sec * rows, rows), rows)

    def hcols(g):
        return pl.ds(pl.multiple_of(g * HEAD, HEAD), HEAD)

    def wcols(g):
        return pl.ds(pl.multiple_of(g * width, HEAD), width)

    def local_in(g):
        return (
            pltpu.make_async_copy(k_hbm.at[0, :, hcols(g)], k_vm.at[g, my_rows, :], kl_sem.at[g]),
            pltpu.make_async_copy(v_hbm.at[0, :, hcols(g)], v_vm.at[g, my_rows, :], vl_sem.at[g]),
            pltpu.make_async_copy(q_hbm.at[0, 0, :, wcols(g)], q_vm.at[g], q_sem.at[g]),
            pltpu.make_async_copy(do_hbm.at[0, 0, :, wcols(g)], do_vm.at[g], do_sem.at[g]),
        )

    def kv_copies(g, off):
        made = []
        for src, dst, ss, rs in ((k_hbm, k_vm, k_ss, k_rs), (v_hbm, v_vm, v_ss, v_rs)):
            made.append(pltpu.make_async_remote_copy(
                src_ref=src.at[0, :, hcols(g)],
                dst_ref=dst.at[g, my_rows, :],
                send_sem=ss.at[off - 1, g],
                recv_sem=rs.at[off - 1, g],
                device_id={"section": sec_peer(off)},
                device_id_type=MESH,
            ))
        return made

    def grad_copy(g, off):
        peer = sec_peer(off)
        return pltpu.make_async_remote_copy(
            src_ref=gsend.at[g, pl.ds(pl.multiple_of(peer * rows, rows), rows), :],
            dst_ref=grecv.at[off - 1, g],
            send_sem=g_ss.at[off - 1, g],
            recv_sem=g_rs.at[off - 1, g],
            device_id={"section": peer},
            device_id_type=MESH,
        )

    def st_copy(s, g, off):
        mine = member(s)
        return pltpu.make_async_remote_copy(
            src_ref=slots[s].at[g, mine],
            dst_ref=slots[s].at[g, mine],
            send_sem=st_ss[s].at[off - 1, g],
            recv_sem=st_rs[s].at[off - 1, g],
            device_id={"dp": st_peer(s, off)},
            device_id_type=MESH,
        )

    def st_total(s, g):
        for off in range(1, stages[s]):
            st_copy(s, g, off).wait_recv()
        total = slots[s][g, 0]
        for m in range(1, stages[s]):
            total = total + slots[s][g, m]
        return total

    def st_send(s, g, value):
        slots[s][g, member(s)] = value
        for off in range(1, stages[s]):
            st_copy(s, g, off).start()

    small = [
        pltpu.make_async_copy(src, dst, small_sem.at[i])
        for i, (src, dst) in enumerate(((doc_hbm, doc_ref), (qs_hbm, qs_ref), (ks_hbm, ks_ref)))
    ]
    for c in small:
        c.start()

    @pl.loop(0, groups)
    def _(g):
        for c in local_in(g):
            c.start()

    for c in small:
        c.wait()
    doc = doc_ref[0]
    j_pos = lax.broadcasted_iota(jnp.int32, (length, length), 0)
    i_pos = lax.broadcasted_iota(jnp.int32, (length, length), 1)
    visible = (j_pos <= i_pos) & ((i_pos < doc) | (j_pos >= doc))
    bias[...] = jnp.where(visible, 0.0, -1e30).astype(F32)

    pl.semaphore_wait(barrier, count)

    @pl.loop(0, groups)
    def _(g):
        for off in range(1, sections):
            for c in kv_copies(g, off):
                c.start()

    def one_group(g, carry):
        for c in local_in(g):
            c.wait()
        for off in range(1, sections):
            for c in kv_copies(g, off):
                c.wait_recv()
        k_scale = ks_ref[:, hcols(g)]
        k_raw = k_vm[g].astype(F32)
        k_f = k_raw * k_scale
        k_low = k_f.astype(BF)
        k_t = k_low.astype(F32).T.astype(BF)
        val = v_vm[g]
        k0, k1 = k_low[:half], k_low[half:]
        v0, v1 = val[:half], val[half:]
        sums = [None] * 4
        gain_rows = []

        def scores(h):
            cols = slice(h * HEAD, (h + 1) * HEAD)
            q_scale = qs_ref[:, pl.ds(pl.multiple_of(g * width + h * HEAD, HEAD), HEAD)]
            q_low = (q_vm[g, :, cols].astype(F32) * q_scale).astype(BF)
            d_out = do_vm[g, :, cols]
            s0 = lax.dot_general(k0, q_low, NT, preferred_element_type=F32)
            s1 = lax.dot_general(k1, q_low[half:], NT, preferred_element_type=F32)
            d0 = lax.dot_general(v0, d_out, NT, preferred_element_type=F32)
            d1 = lax.dot_general(v1, d_out[half:], NT, preferred_element_type=F32)
            return q_low, s0, s1, d0, d1

        def softmax(s0, s1, d0, d1):
            s0 = s0 + bias[:half, :]
            s1 = s1 + bias[half:, half:]
            m0 = jnp.max(s0, axis=0, keepdims=True)
            m1 = jnp.max(s1, axis=0, keepdims=True)
            m_b = jnp.maximum(m0[:, half:], m1)
            m0 = jnp.concatenate([m0[:, :half], m_b], axis=1)
            e0 = jnp.exp2((s0 - m0) * to_exp2)
            e1 = jnp.exp2((s1 - m_b) * to_exp2)
            t0 = jnp.sum(e0, axis=0, keepdims=True)
            t1 = jnp.sum(e1, axis=0, keepdims=True)
            t0 = jnp.concatenate([t0[:, :half], t0[:, half:] + t1], axis=1)
            inv = 1.0 / t0
            p0 = e0 * inv
            p1 = e1 * inv[:, half:]
            r0 = jnp.sum(p0 * d0, axis=0, keepdims=True)
            r1 = jnp.sum(p1 * d1, axis=0, keepdims=True)
            r0 = jnp.concatenate([r0[:, :half], r0[:, half:] + r1], axis=1)
            ds0 = (p0 * (d0 - r0) * scale).astype(BF)
            ds1 = (p1 * (d1 - r0[:, half:]) * scale).astype(BF)
            return p0.astype(BF), p1.astype(BF), ds0, ds1

        def grads(h, q_low, p0_low, p1_low, ds0, ds1):
            cols = slice(h * HEAD, (h + 1) * HEAD)
            q_scale = qs_ref[:, pl.ds(pl.multiple_of(g * width + h * HEAD, HEAD), HEAD)]
            d_out = do_vm[g, :, cols]
            made = (
                jnp.dot(p0_low, d_out, preferred_element_type=F32),
                jnp.dot(p1_low, d_out[half:], preferred_element_type=F32),
                jnp.dot(ds0, q_low, preferred_element_type=F32),
                jnp.dot(ds1, q_low[half:], preferred_element_type=F32),
            )
            for i, x in enumerate(made):
                sums[i] = x if h == 0 else sums[i] + x
            ds_full = jnp.concatenate(
                [ds0, jnp.concatenate([jnp.zeros((half, half), BF), ds1], axis=1)], axis=0
            )
            dq = jnp.dot(k_t, ds_full, preferred_element_type=F32).T
            dq_ref[0, 0, :, pl.ds(pl.multiple_of(g * width + h * HEAD, HEAD), HEAD)] = (dq * q_scale).astype(BF)
            gain_rows.append(jnp.sum(dq * q_vm[g, :, cols].astype(F32), axis=0, keepdims=True))

        ahead = scores(0)
        for h in range(per):
            q_low, *sd = ahead
            if h + 1 < per:
                ahead = scores(h + 1)
            grads(h, q_low, *softmax(*sd))
        dv0, dv1, dk0, dk1 = sums
        dk = jnp.concatenate([dk0, dk1], axis=0)
        dv = jnp.concatenate([dv0, dv1], axis=0)
        key_term = dk * k_scale
        grad[g, :, :HEAD] = key_term
        grad[g, :, HEAD:] = dv
        gsend[g, :, :HEAD] = key_term.astype(BF)
        gsend[g, :, HEAD:] = dv.astype(BF)
        for off in range(1, sections):
            grad_copy(g, off).start()
        gain_rows.append(jnp.sum(dk * k_raw, axis=0, keepdims=True))
        spare = slots[0].shape[2] - len(gain_rows)
        if spare:
            gain_rows.append(jnp.zeros((spare, HEAD), F32))
        st_send(0, g, jnp.concatenate(gain_rows, axis=0))
        for s in range(1, n_st):
            @pl.when(g >= LAG * s)
            def _():
                st_send(s, g - LAG * s, st_total(s - 1, g - LAG * s))
        return carry

    lax.fori_loop(0, groups, one_group, 0)

    def finish_gain(g):
        total = st_total(n_st - 1, g) * (1.0 / replicas)
        for h in range(per):
            qgain_ref[:, (g * per + h) * HEAD:(g * per + h + 1) * HEAD] = total[h:h + 1]
        kgain_ref[:, g * HEAD:(g + 1) * HEAD] = total[per:per + 1]

    def finish_grad(g):
        total = grad[g, my_rows, :]
        for off in range(1, sections):
            grad_copy(g, off).wait_recv()
            total = total + grecv[off - 1, g].astype(F32)
        kg_ref[0, :, g * HEAD:(g + 1) * HEAD] = total[:, :HEAD].astype(BF)
        vg_ref[0, :, g * HEAD:(g + 1) * HEAD] = total[:, HEAD:].astype(BF)

    for t in range(groups, groups + LAG * (n_st - 1)):
        for s in range(n_st - 1, 0, -1):
            g = t - LAG * s
            if 0 <= g < groups:
                st_send(s, g, st_total(s - 1, g))
    for g in range(groups):
        finish_grad(g)
    for g in range(groups):
        finish_gain(g)

    @pl.loop(0, groups)
    def _(g):
        for off in range(1, sections):
            for c in kv_copies(g, off):
                c.wait_send()
            grad_copy(g, off).wait_send()
        for s in range(n_st):
            for off in range(1, stages[s]):
                st_copy(s, g, off).wait_send()


def write_out(*refs):
    n = len(refs) // 2
    sems = refs[-1]
    copies = [pltpu.make_async_copy(refs[i], refs[n + i], sems.at[i]) for i in range(n)]
    for c in copies:
        c.start()
    for c in copies:
        c.wait()


def solution(mesh):
    sections = mesh.shape["section"]
    replicas = mesh.shape["dp"]
    stages = radices(replicas)

    def on_device(queries, keys, values, query_gain, key_channel_scale, out_grad, doc_start):
        length = queries.shape[2]
        rows, kv_width = keys.shape[1], keys.shape[2]
        groups = kv_width // HEAD
        width = queries.shape[3] // groups
        gain_rows = -(-(width // HEAD + 1) // 8) * 8
        vmem = pl.BlockSpec(memory_space=pltpu.VMEM)
        hbm = pl.BlockSpec(memory_space=pl.ANY)
        dma = pltpu.SemaphoreType.DMA
        peers = sections - 1
        scratch = [
            pltpu.SMEM(doc_start.shape, jnp.int32),
            pltpu.VMEM(query_gain.shape, F32),
            pltpu.VMEM(key_channel_scale.shape, F32),
            pltpu.VMEM((groups, length, width), BF),
            pltpu.VMEM((groups, length, width), BF),
            pltpu.VMEM((groups, length, HEAD), BF),
            pltpu.VMEM((groups, length, HEAD), BF),
            pltpu.VMEM((length, length), F32),
            pltpu.VMEM((groups, length, 2 * HEAD), F32),
            pltpu.VMEM((groups, length, 2 * HEAD), BF),
            pltpu.VMEM((peers, groups, rows, 2 * HEAD), BF),
        ]
        scratch += [pltpu.VMEM((groups, r, gain_rows, HEAD), F32) for r in stages]
        scratch += [dma((3,))] + [dma((groups,))] * 4
        scratch += [dma((peers, groups))] * 6
        scratch += [dma((r - 1, groups)) for r in stages] * 2
        shapes = (
            jax.ShapeDtypeStruct(queries.shape, BF),
            jax.ShapeDtypeStruct(keys.shape, BF),
            jax.ShapeDtypeStruct(values.shape, BF),
            jax.ShapeDtypeStruct(query_gain.shape, F32),
            jax.ShapeDtypeStruct(key_channel_scale.shape, F32),
        )
        held = pl.pallas_call(
            functools.partial(kernel, sections, replicas, stages),
            out_shape=tuple(pltpu.VMEM(x.shape, x.dtype) for x in shapes),
            in_specs=[pl.BlockSpec(memory_space=pltpu.HBM)] + [hbm] * 6,
            out_specs=(vmem,) * 5,
            scratch_shapes=scratch,
            compiler_params=pltpu.CompilerParams(collective_id=0, has_side_effects=True),
        )(doc_start, queries, keys, values, query_gain, key_channel_scale, out_grad)
        return pl.pallas_call(
            write_out,
            out_shape=shapes,
            in_specs=[vmem] * 5,
            out_specs=(hbm,) * 5,
            scratch_shapes=[dma((5,))],
        )(*[pltpu.with_memory_space_constraint(x, pltpu.VMEM) for x in held])

    in_specs = (
        P("section", "dp", None, None),
        P("dp", "section", None),
        P("dp", "section", None),
        P("section", None),
        P("section", None),
        P("section", "dp", None, None),
        P("dp"),
    )
    out_specs = (
        P("section", "dp", None, None),
        P("dp", "section", None),
        P("dp", "section", None),
        P("section", None),
        P("section", None),
    )
    return jax.shard_map(
        on_device, mesh=mesh, in_specs=in_specs, out_specs=out_specs, check_vma=False
    )
```

profile of v0, /device:TPU:0, one launch (start us, length us, event | category | flops | bytes accessed | tf_op | source)
XLA Modules:
  0.0 26.3 jit_solution(10898473054850378894)
XLA Ops:
  1.3 23.9 %shard_map.110 = (bf16[1,1,256,2560]{3,2,1,0:T(8,128)(2,1)S(1)}, bf16[1,128,512]{2,1,0:T(8,128)(2,1)S(1)}, bf16[1,128,512]{2,1,0:T(8,128)(2,1)S(1)}, f32[1,2560]{1,0:T(1,128)S(1)}, f32[1,512]{1,0:T(1,128)S(1)}) custom-call(s32[1]{0:T(128)S(6)} %copy.12.doc_hbm, bf16[1,1,256,2560]{3,2,1,0:T(8,128)(2,1)} %q_hbm.1, bf16[1,128,512]{2,1,0:T(8,128)(2,1)} %k_hbm.1, ...), custom_call_target="tpu_custom_call" | custom-call | tf_op jit(solution)/shard_map/pallas_call | solution.py:351
  25.1 1.2 %shard_map.111 = (bf16[1,1,256,2560]{3,2,1,0:T(8,128)(2,1)}, bf16[1,128,512]{2,1,0:T(8,128)(2,1)}, bf16[1,128,512]{2,1,0:T(8,128)(2,1)}, f32[1,2560]{1,0:T(1,128)}, f32[1,512]{1,0:T(1,128)}) custom-call(bf16[1,1,256,2560]{3,2,1,0:T(8,128)(2,1)S(1)} %get-tuple-element.10.refs_0_, bf16[1,128,512]{2,1,0:T(8,128)(2,1)S(1)} %get-tuple-element.11.refs_1_, ...), custom_call_target="tpu_custom_call" | custom-call | tf_op jit(solution)/shard_map/pallas_call | solution.py:359
where the time goes:
time: 26.6 us; the launch traced here: 26.3 us
  Pallas kernels  25 us (94%)
  between operations  1.29 us (5%)
    pallas_call x1, Pallas kernels, on_device(): pl.pallas_call(functools.partial(kernel, sections, replicas, stages), out...  23.9 us
    pallas_call x1, Pallas kernels, on_device(): pl.pallas_call(write_out, out_shape=shapes, in_specs=[vmem] * 5, out_spec...  1.18 us

commit v1 on v0

--- a/solution.py
+++ b/solution.py
@@ -10,6 +10,8 @@
 
 HEAD = 128
 LAG = 2
+DIRECT = 16
+NEAR = 4
 MESH = pl.DeviceIdType.MESH
 BF = jnp.bfloat16
 F32 = jnp.float32
@@ -18,13 +20,17 @@
 
 def radices(n):
     out = []
-    for r in (4, 3, 2, 5, 7):
-        while n % r == 0:
-            out.append(r)
-            n //= r
-    if n > 1:
-        out.append(n)
+    while n > 1:
+        r = next((r for r in range(DIRECT, 1, -1) if n % r == 0), n)
+        out.append(r)
+        n //= r
     return out
+
+
+def near_split(stages):
+    if len(stages) == 1 and stages[0] % NEAR == 0:
+        return NEAR, stages[0] // NEAR
+    return 0, 0
 
 
 def kernel(
@@ -35,9 +41,10 @@
 ):
     n_st = len(stages)
     slots = rest[:n_st]
-    (small_sem, q_sem, do_sem, kl_sem, vl_sem, k_ss, k_rs, v_ss, v_rs, g_ss, g_rs) = rest[n_st:n_st + 11]
-    st_ss = rest[n_st + 11:2 * n_st + 11]
-    st_rs = rest[2 * n_st + 11:]
+    (small_sem, q_sem, do_sem, kl_sem, vl_sem, kv_ss, kv_rs, g_ss, g_rs) = rest[n_st:n_st + 9]
+    st_ss = rest[n_st + 9:2 * n_st + 9]
+    st_rs = rest[2 * n_st + 9:3 * n_st + 9]
+    line_sems = rest[3 * n_st + 9:]
     groups, length, width = q_vm.shape
     per = width // HEAD
     rows = k_hbm.shape[1]
@@ -64,15 +71,37 @@
         other = lax.rem(mine + off, stages[s])
         return dp + (other - mine) * strides[s]
 
+    near, far = near_split(stages)
+    row = dp // near if near else 0
+
+    def line_signal(sem):
+        @pl.when(row > 0)
+        def _():
+            pl.semaphore_signal(sem, inc=1, device_id={"dp": dp - near}, device_id_type=MESH)
+
+        @pl.when(row < far - 1)
+        def _():
+            pl.semaphore_signal(sem, inc=1, device_id={"dp": dp + near}, device_id_type=MESH)
+
+    line_count = jnp.where(row > 0, 1, 0) + jnp.where(row < far - 1, 1, 0)
     barrier = pltpu.get_barrier_semaphore()
     count = 0
     for off in range(1, sections):
         pl.semaphore_signal(barrier, inc=1, device_id={"section": sec_peer(off)}, device_id_type=MESH)
         count += 1
-    for s in range(n_st):
-        for off in range(1, stages[s]):
-            pl.semaphore_signal(barrier, inc=1, device_id={"dp": st_peer(s, off)}, device_id_type=MESH)
+    if near:
+        for off in range(1, near):
+            other = row * near + lax.rem(lax.rem(dp, near) + off, near)
+            pl.semaphore_signal(barrier, inc=1, device_id={"dp": other}, device_id_type=MESH)
             count += 1
+        if far > 1:
+            line_signal(barrier)
+            count = count + line_count
+    else:
+        for s in range(n_st):
+            for off in range(1, stages[s]):
+                pl.semaphore_signal(barrier, inc=1, device_id={"dp": st_peer(s, off)}, device_id_type=MESH)
+                count += 1
 
     my_rows = pl.ds(pl.multiple_of(sec * rows, rows), rows)
 
@@ -92,12 +121,12 @@
 
     def kv_copies(g, off):
         made = []
-        for src, dst, ss, rs in ((k_hbm, k_vm, k_ss, k_rs), (v_hbm, v_vm, v_ss, v_rs)):
+        for src, dst in ((k_hbm, k_vm), (v_hbm, v_vm)):
             made.append(pltpu.make_async_remote_copy(
                 src_ref=src.at[0, :, hcols(g)],
                 dst_ref=dst.at[g, my_rows, :],
-                send_sem=ss.at[off - 1, g],
-                recv_sem=rs.at[off - 1, g],
+                send_sem=kv_ss.at[off - 1],
+                recv_sem=kv_rs.at[off - 1, g],
                 device_id={"section": sec_peer(off)},
                 device_id_type=MESH,
             ))
@@ -108,7 +137,7 @@
         return pltpu.make_async_remote_copy(
             src_ref=gsend.at[g, pl.ds(pl.multiple_of(peer * rows, rows), rows), :],
             dst_ref=grecv.at[off - 1, g],
-            send_sem=g_ss.at[off - 1, g],
+            send_sem=g_ss.at[off - 1],
             recv_sem=g_rs.at[off - 1, g],
             device_id={"section": peer},
             device_id_type=MESH,
@@ -119,24 +148,29 @@
         return pltpu.make_async_remote_copy(
             src_ref=slots[s].at[g, mine],
             dst_ref=slots[s].at[g, mine],
-            send_sem=st_ss[s].at[off - 1, g],
-            recv_sem=st_rs[s].at[off - 1, g],
+            send_sem=st_ss[s],
+            recv_sem=st_rs[s].at[g],
             device_id={"dp": st_peer(s, off)},
             device_id_type=MESH,
         )
 
+    def drain(ref, sem):
+        pltpu.make_async_copy(ref, ref, sem).wait()
+
     def st_total(s, g):
-        for off in range(1, stages[s]):
-            st_copy(s, g, off).wait_recv()
+        drain(slots[s].at[g, :stages[s] - 1], st_rs[s].at[g])
         total = slots[s][g, 0]
         for m in range(1, stages[s]):
             total = total + slots[s][g, m]
         return total
 
+    def st_start(s, g):
+        for off in range(1, stages[s]):
+            st_copy(s, g, off).start()
+
     def st_send(s, g, value):
         slots[s][g, member(s)] = value
-        for off in range(1, stages[s]):
-            st_copy(s, g, off).start()
+        st_start(s, g)
 
     small = [
         pltpu.make_async_copy(src, dst, small_sem.at[i])
@@ -149,6 +183,17 @@
     def _(g):
         for c in local_in(g):
             c.start()
+
+    pl.semaphore_wait(barrier, count)
+
+    @pl.loop(0, groups)
+    def _(g):
+        for off in range(1, sections):
+            for c in kv_copies(g, off):
+                c.start()
+
+    if line_sems:
+        line_signal(line_sems[0])
 
     for c in small:
         c.wait()
@@ -158,20 +203,11 @@
     visible = (j_pos <= i_pos) & ((i_pos < doc) | (j_pos >= doc))
     bias[...] = jnp.where(visible, 0.0, -1e30).astype(F32)
 
-    pl.semaphore_wait(barrier, count)
-
-    @pl.loop(0, groups)
-    def _(g):
-        for off in range(1, sections):
-            for c in kv_copies(g, off):
-                c.start()
-
     def one_group(g, carry):
         for c in local_in(g):
             c.wait()
         for off in range(1, sections):
-            for c in kv_copies(g, off):
-                c.wait_recv()
+            drain(grecv.at[off - 1, g], kv_rs.at[off - 1, g])
         k_scale = ks_ref[:, hcols(g)]
         k_raw = k_vm[g].astype(F32)
         k_f = k_raw * k_scale
@@ -255,7 +291,25 @@
         spare = slots[0].shape[2] - len(gain_rows)
         if spare:
             gain_rows.append(jnp.zeros((spare, HEAD), F32))
-        st_send(0, g, jnp.concatenate(gain_rows, axis=0))
+        gain_block = jnp.concatenate(gain_rows, axis=0)
+        slots[0][g, member(0)] = gain_block
+        for i in range(len(line_sems)):
+            @pl.when(g == i)
+            def _():
+                pl.semaphore_wait(line_sems[i], line_count)
+                if i + 1 < len(line_sems):
+                    line_signal(line_sems[i + 1])
+        hold = max(len(line_sems) - 1, 0)
+
+        @pl.when(g == hold)
+        def _():
+            for e in range(hold):
+                st_start(0, e)
+
+        @pl.when(g >= hold)
+        def _():
+            st_start(0, g)
+
         for s in range(1, n_st):
             @pl.when(g >= LAG * s)
             def _():
@@ -288,15 +342,11 @@
     for g in range(groups):
         finish_gain(g)
 
-    @pl.loop(0, groups)
-    def _(g):
-        for off in range(1, sections):
-            for c in kv_copies(g, off):
-                c.wait_send()
-            grad_copy(g, off).wait_send()
-        for s in range(n_st):
-            for off in range(1, stages[s]):
-                st_copy(s, g, off).wait_send()
+    for off in range(1, sections):
+        drain(grecv.at[off - 1], kv_ss.at[off - 1])
+        drain(grecv.at[off - 1], g_ss.at[off - 1])
+    for s in range(n_st):
+        drain(slots[s].at[:, :stages[s] - 1], st_ss[s])
 
 
 def write_out(*refs):
@@ -313,6 +363,7 @@
     sections = mesh.shape["section"]
     replicas = mesh.shape["dp"]
     stages = radices(replicas)
+    n_st = len(stages)
 
     def on_device(queries, keys, values, query_gain, key_channel_scale, out_grad, doc_start):
         length = queries.shape[2]
@@ -339,8 +390,9 @@
         ]
         scratch += [pltpu.VMEM((groups, r, gain_rows, HEAD), F32) for r in stages]
         scratch += [dma((3,))] + [dma((groups,))] * 4
-        scratch += [dma((peers, groups))] * 6
-        scratch += [dma((r - 1, groups)) for r in stages] * 2
+        scratch += [dma((peers,)), dma((peers, groups))] * 2
+        scratch += [dma] * n_st + [dma((groups,))] * n_st
+        scratch += [pltpu.SemaphoreType.REGULAR] * max(near_split(stages)[1] - 1, 0)
         shapes = (
             jax.ShapeDtypeStruct(queries.shape, BF),
             jax.ShapeDtypeStruct(keys.shape, BF),

time: 26.6 us -> 24.5 us (0.921)
  Pallas kernels: 25 us -> 23.1 us
    pallas_call x1, Pallas kernels: 23.9 us -> 21.9 us  [on_device(): pl.pallas_call(functools.partial(kernel, sections, replicas, stages), out...]
where the time goes in v1:
time: 24.5 us; the launch traced here: 24.3 us
  Pallas kernels  23.1 us (94%)
  between operations  1.29 us (5%)
    pallas_call x1, Pallas kernels, on_device(): pl.pallas_call(functools.partial(kernel, sections, replicas, stages), out...  21.9 us
    pallas_call x1, Pallas kernels, on_device(): pl.pallas_call(write_out, out_shape=shapes, in_specs=[vmem] * 5, out_spec...  1.18 us

profile of v1, /device:TPU:0, one launch (start us, length us, event | category | flops | bytes accessed | tf_op | source)
XLA Modules:
  0.0 24.3 jit_solution(11394335088853050283)
XLA Ops:
  1.3 21.9 %shard_map.110 = (bf16[1,1,256,2560]{3,2,1,0:T(8,128)(2,1)S(1)}, bf16[1,128,512]{2,1,0:T(8,128)(2,1)S(1)}, bf16[1,128,512]{2,1,0:T(8,128)(2,1)S(1)}, f32[1,2560]{1,0:T(1,128)S(1)}, f32[1,512]{1,0:T(1,128)S(1)}) custom-call(s32[1]{0:T(128)S(6)} %copy.12.doc_hbm, bf16[1,1,256,2560]{3,2,1,0:T(8,128)(2,1)} %q_hbm.1, bf16[1,128,512]{2,1,0:T(8,128)(2,1)} %k_hbm.1, ...), custom_call_target="tpu_custom_call" | custom-call | tf_op jit(solution)/shard_map/pallas_call | solution.py:403
  23.2 1.2 %shard_map.111 = (bf16[1,1,256,2560]{3,2,1,0:T(8,128)(2,1)}, bf16[1,128,512]{2,1,0:T(8,128)(2,1)}, bf16[1,128,512]{2,1,0:T(8,128)(2,1)}, f32[1,2560]{1,0:T(1,128)}, f32[1,512]{1,0:T(1,128)}) custom-call(bf16[1,1,256,2560]{3,2,1,0:T(8,128)(2,1)S(1)} %get-tuple-element.10.refs_0_, bf16[1,128,512]{2,1,0:T(8,128)(2,1)S(1)} %get-tuple-element.11.refs_1_, ...), custom_call_target="tpu_custom_call" | custom-call | tf_op jit(solution)/shard_map/pallas_call | solution.py:411

commit v2 on v1

--- a/solution.py
+++ b/solution.py
@@ -37,7 +37,7 @@
     sections, replicas, stages,
     doc_hbm, q_hbm, k_hbm, v_hbm, qs_hbm, ks_hbm, do_hbm,
     dq_ref, kg_ref, vg_ref, qgain_ref, kgain_ref,
-    doc_ref, qs_ref, ks_ref, q_vm, do_vm, k_vm, v_vm, bias, grad, gsend, grecv, *rest,
+    doc_ref, qs_ref, ks_ref, q_vm, do_vm, k_vm, v_vm, ql_vm, qf_vm, sbuf, dbuf, pbuf, dsbuf, bias, grad, gsend, grecv, *rest,
 ):
     n_st = len(stages)
     slots = rest[:n_st]
@@ -115,9 +115,11 @@
         return (
             pltpu.make_async_copy(k_hbm.at[0, :, hcols(g)], k_vm.at[g, my_rows, :], kl_sem.at[g]),
             pltpu.make_async_copy(v_hbm.at[0, :, hcols(g)], v_vm.at[g, my_rows, :], vl_sem.at[g]),
-            pltpu.make_async_copy(q_hbm.at[0, 0, :, wcols(g)], q_vm.at[g], q_sem.at[g]),
             pltpu.make_async_copy(do_hbm.at[0, 0, :, wcols(g)], do_vm.at[g], do_sem.at[g]),
         )
+
+    def q_in(g):
+        return pltpu.make_async_copy(q_hbm.at[0, 0, :, wcols(g)], q_vm.at[g], q_sem.at[g])
 
     def kv_copies(g, off):
         made = []
@@ -181,6 +183,7 @@
 
     @pl.loop(0, groups)
     def _(g):
+        q_in(g).start()
         for c in local_in(g):
             c.start()
 
@@ -201,7 +204,19 @@
     j_pos = lax.broadcasted_iota(jnp.int32, (length, length), 0)
     i_pos = lax.broadcasted_iota(jnp.int32, (length, length), 1)
     visible = (j_pos <= i_pos) & ((i_pos < doc) | (j_pos >= doc))
-    bias[...] = jnp.where(visible, 0.0, -1e30).astype(F32)
+    shade = jnp.where(visible, 0.0, -1e30).astype(F32)
+    bias[0] = shade[:half, :half]
+    bias[1] = shade[:half, half:]
+    bias[2] = shade[half:, half:]
+
+    @pl.loop(0, groups)
+    def _(g):
+        q_in(g).wait()
+        for h in range(per):
+            q_f = q_vm[g, :, h * HEAD:(h + 1) * HEAD].astype(F32)
+            q_scale = qs_ref[:, pl.ds(pl.multiple_of(g * width + h * HEAD, HEAD), HEAD)]
+            qf_vm[g, h] = q_f
+            ql_vm[g, h] = (q_f * q_scale).astype(BF)
 
     def one_group(g, carry):
         for c in local_in(g):
@@ -210,81 +225,90 @@
             drain(grecv.at[off - 1, g], kv_rs.at[off - 1, g])
         k_scale = ks_ref[:, hcols(g)]
         k_raw = k_vm[g].astype(F32)
-        k_f = k_raw * k_scale
-        k_low = k_f.astype(BF)
+        k_low = (k_raw * k_scale).astype(BF)
         k_t = k_low.astype(F32).T.astype(BF)
         val = v_vm[g]
         k0, k1 = k_low[:half], k_low[half:]
         v0, v1 = val[:half], val[half:]
-        sums = [None] * 4
         gain_rows = []
 
+        def d_out_of(h):
+            return do_vm[g, :, h * HEAD:(h + 1) * HEAD]
+
         def scores(h):
-            cols = slice(h * HEAD, (h + 1) * HEAD)
-            q_scale = qs_ref[:, pl.ds(pl.multiple_of(g * width + h * HEAD, HEAD), HEAD)]
-            q_low = (q_vm[g, :, cols].astype(F32) * q_scale).astype(BF)
-            d_out = do_vm[g, :, cols]
-            s0 = lax.dot_general(k0, q_low, NT, preferred_element_type=F32)
-            s1 = lax.dot_general(k1, q_low[half:], NT, preferred_element_type=F32)
-            d0 = lax.dot_general(v0, d_out, NT, preferred_element_type=F32)
-            d1 = lax.dot_general(v1, d_out[half:], NT, preferred_element_type=F32)
-            return q_low, s0, s1, d0, d1
-
-        def softmax(s0, s1, d0, d1):
-            s0 = s0 + bias[:half, :]
-            s1 = s1 + bias[half:, half:]
-            m0 = jnp.max(s0, axis=0, keepdims=True)
-            m1 = jnp.max(s1, axis=0, keepdims=True)
-            m_b = jnp.maximum(m0[:, half:], m1)
-            m0 = jnp.concatenate([m0[:, :half], m_b], axis=1)
-            e0 = jnp.exp2((s0 - m0) * to_exp2)
-            e1 = jnp.exp2((s1 - m_b) * to_exp2)
-            t0 = jnp.sum(e0, axis=0, keepdims=True)
-            t1 = jnp.sum(e1, axis=0, keepdims=True)
-            t0 = jnp.concatenate([t0[:, :half], t0[:, half:] + t1], axis=1)
-            inv = 1.0 / t0
-            p0 = e0 * inv
-            p1 = e1 * inv[:, half:]
-            r0 = jnp.sum(p0 * d0, axis=0, keepdims=True)
-            r1 = jnp.sum(p1 * d1, axis=0, keepdims=True)
-            r0 = jnp.concatenate([r0[:, :half], r0[:, half:] + r1], axis=1)
-            ds0 = (p0 * (d0 - r0) * scale).astype(BF)
-            ds1 = (p1 * (d1 - r0[:, half:]) * scale).astype(BF)
-            return p0.astype(BF), p1.astype(BF), ds0, ds1
-
-        def grads(h, q_low, p0_low, p1_low, ds0, ds1):
-            cols = slice(h * HEAD, (h + 1) * HEAD)
-            q_scale = qs_ref[:, pl.ds(pl.multiple_of(g * width + h * HEAD, HEAD), HEAD)]
-            d_out = do_vm[g, :, cols]
-            made = (
-                jnp.dot(p0_low, d_out, preferred_element_type=F32),
-                jnp.dot(p1_low, d_out[half:], preferred_element_type=F32),
-                jnp.dot(ds0, q_low, preferred_element_type=F32),
-                jnp.dot(ds1, q_low[half:], preferred_element_type=F32),
+            q_low = ql_vm[g, h]
+            x = lax.dot_general(k0, q_low, NT, preferred_element_type=F32)
+            sbuf[h % 2, 0], sbuf[h % 2, 1] = x[:, :half], x[:, half:]
+            sbuf[h % 2, 2] = lax.dot_general(k1, q_low[half:], NT, preferred_element_type=F32)
+
+        def d_probs(h):
+            d_out = d_out_of(h)
+            x = lax.dot_general(v0, d_out, NT, preferred_element_type=F32)
+            dbuf[h % 2, 0], dbuf[h % 2, 1] = x[:, :half], x[:, half:]
+            dbuf[h % 2, 2] = lax.dot_general(v1, d_out[half:], NT, preferred_element_type=F32)
+
+        def softmax(h, blocks):
+            b = h % 2
+            xs = [sbuf[b, i] + bias[i] for i in blocks]
+            top = functools.reduce(jnp.maximum, xs)
+            top = jnp.max(top, axis=0, keepdims=True)
+            es = [jnp.exp2((x - top) * to_exp2) for x in xs]
+            inv = 1.0 / jnp.sum(functools.reduce(jnp.add, es), axis=0, keepdims=True)
+            ps = [e * inv for e in es]
+            r = [p * dbuf[b, i] for p, i in zip(ps, blocks)]
+            r = jnp.sum(functools.reduce(jnp.add, r), axis=0, keepdims=True)
+            for p, i in zip(ps, blocks):
+                pbuf[b, i] = p.astype(BF)
+                dsbuf[b, i] = (p * (dbuf[b, i] - r)).astype(BF)
+
+        def wide(ref, h):
+            return jnp.concatenate([ref[h % 2, 0], ref[h % 2, 1]], axis=1)
+
+        def add(h, rows_, cols_, x):
+            if h == 0:
+                grad[g, rows_, cols_] = x
+            else:
+                grad[g, rows_, cols_] += x
+
+        lo, hi = slice(0, half), slice(half, 2 * half)
+        kc, vc = slice(0, HEAD), slice(HEAD, 2 * HEAD)
+
+        def kv_grads(h):
+            d_out, q_low = d_out_of(h), ql_vm[g, h]
+            add(h, lo, vc, jnp.dot(wide(pbuf, h), d_out, preferred_element_type=F32))
+            add(h, hi, vc, jnp.dot(pbuf[h % 2, 2], d_out[half:], preferred_element_type=F32))
+            add(h, lo, kc, jnp.dot(wide(dsbuf, h), q_low, preferred_element_type=F32))
+            add(h, hi, kc, jnp.dot(dsbuf[h % 2, 2], q_low[half:], preferred_element_type=F32))
+
+        def q_grads(h):
+            ds_full = jnp.concatenate(
+                [wide(dsbuf, h), jnp.concatenate([jnp.zeros((half, half), BF), dsbuf[h % 2, 2]], axis=1)], axis=0
             )
-            for i, x in enumerate(made):
-                sums[i] = x if h == 0 else sums[i] + x
-            ds_full = jnp.concatenate(
-                [ds0, jnp.concatenate([jnp.zeros((half, half), BF), ds1], axis=1)], axis=0
-            )
+            cols = pl.ds(pl.multiple_of(g * width + h * HEAD, HEAD), HEAD)
             dq = jnp.dot(k_t, ds_full, preferred_element_type=F32).T
-            dq_ref[0, 0, :, pl.ds(pl.multiple_of(g * width + h * HEAD, HEAD), HEAD)] = (dq * q_scale).astype(BF)
-            gain_rows.append(jnp.sum(dq * q_vm[g, :, cols].astype(F32), axis=0, keepdims=True))
-
-        ahead = scores(0)
+            dq_ref[0, 0, :, cols] = (dq * (qs_ref[:, cols] * scale)).astype(BF)
+            gain_rows.append(jnp.sum(dq * qf_vm[g, h], axis=0, keepdims=True))
+
+        scores(0)
+        d_probs(0)
         for h in range(per):
-            q_low, *sd = ahead
             if h + 1 < per:
-                ahead = scores(h + 1)
-            grads(h, q_low, *softmax(*sd))
-        dv0, dv1, dk0, dk1 = sums
-        dk = jnp.concatenate([dk0, dk1], axis=0)
-        dv = jnp.concatenate([dv0, dv1], axis=0)
-        key_term = dk * k_scale
+                scores(h + 1)
+            softmax(h, (0,))
+            if h + 1 < per:
+                d_probs(h + 1)
+            if h:
+                kv_grads(h - 1)
+            softmax(h, (1, 2))
+            if h:
+                q_grads(h - 1)
+        kv_grads(per - 1)
+        q_grads(per - 1)
+        dk = grad[g, :, :HEAD]
+        key_term = dk * (k_scale * scale)
         grad[g, :, :HEAD] = key_term
-        grad[g, :, HEAD:] = dv
         gsend[g, :, :HEAD] = key_term.astype(BF)
-        gsend[g, :, HEAD:] = dv.astype(BF)
+        gsend[g, :, HEAD:] = grad[g, :, HEAD:].astype(BF)
         for off in range(1, sections):
             grad_copy(g, off).start()
         gain_rows.append(jnp.sum(dk * k_raw, axis=0, keepdims=True))
@@ -319,7 +343,7 @@
     lax.fori_loop(0, groups, one_group, 0)
 
     def finish_gain(g):
-        total = st_total(n_st - 1, g) * (1.0 / replicas)
+        total = st_total(n_st - 1, g) * (scale / replicas)
         for h in range(per):
             qgain_ref[:, (g * per + h) * HEAD:(g * per + h + 1) * HEAD] = total[h:h + 1]
         kgain_ref[:, g * HEAD:(g + 1) * HEAD] = total[per:per + 1]
@@ -368,7 +392,7 @@
     def on_device(queries, keys, values, query_gain, key_channel_scale, out_grad, doc_start):
         length = queries.shape[2]
         rows, kv_width = keys.shape[1], keys.shape[2]
-        groups = kv_width // HEAD
+        groups, half = kv_width // HEAD, length // 2
         width = queries.shape[3] // groups
         gain_rows = -(-(width // HEAD + 1) // 8) * 8
         vmem = pl.BlockSpec(memory_space=pltpu.VMEM)
@@ -383,7 +407,13 @@
             pltpu.VMEM((groups, length, width), BF),
             pltpu.VMEM((groups, length, HEAD), BF),
             pltpu.VMEM((groups, length, HEAD), BF),
-            pltpu.VMEM((length, length), F32),
+            pltpu.VMEM((groups, width // HEAD, length, HEAD), BF),
+            pltpu.VMEM((groups, width // HEAD, length, HEAD), F32),
+            pltpu.VMEM((2, 3, half, half), F32),
+            pltpu.VMEM((2, 3, half, half), F32),
+            pltpu.VMEM((2, 3, half, half), BF),
+            pltpu.VMEM((2, 3, half, half), BF),
+            pltpu.VMEM((3, half, half), F32),
             pltpu.VMEM((groups, length, 2 * HEAD), F32),
             pltpu.VMEM((groups, length, 2 * HEAD), BF),
             pltpu.VMEM((peers, groups, rows, 2 * HEAD), BF),

time: 24.5 us -> 22.6 us (0.922)
  Pallas kernels: 23.1 us -> 21.1 us
    pallas_call x1, Pallas kernels: 21.9 us -> 20 us  [on_device(): pl.pallas_call(functools.partial(kernel, sections, replicas, stages), out...]
where the time goes in v2:
time: 22.6 us; the launch traced here: 22.4 us
  Pallas kernels  21.1 us (93%)
  between operations  1.29 us (6%)
    pallas_call x1, Pallas kernels, on_device(): pl.pallas_call(functools.partial(kernel, sections, replicas, stages), out...  20 us
    pallas_call x1, Pallas kernels, on_device(): pl.pallas_call(write_out, out_shape=shapes, in_specs=[vmem] * 5, out_spec...  1.18 us

profile of v2, /device:TPU:0, one launch (start us, length us, event | category | flops | bytes accessed | tf_op | source)
XLA Modules:
  0.0 22.4 jit_solution(9627103814469198424)
XLA Ops:
  1.3 20.0 %shard_map.110 = (bf16[1,1,256,2560]{3,2,1,0:T(8,128)(2,1)S(1)}, bf16[1,128,512]{2,1,0:T(8,128)(2,1)S(1)}, bf16[1,128,512]{2,1,0:T(8,128)(2,1)S(1)}, f32[1,2560]{1,0:T(1,128)S(1)}, f32[1,512]{1,0:T(1,128)S(1)}) custom-call(s32[1]{0:T(128)S(6)} %copy.12.doc_hbm, bf16[1,1,256,2560]{3,2,1,0:T(8,128)(2,1)} %q_hbm.1, bf16[1,128,512]{2,1,0:T(8,128)(2,1)} %k_hbm.1, ...), custom_call_target="tpu_custom_call" | custom-call | tf_op jit(solution)/shard_map/pallas_call | solution.py:433
  21.2 1.2 %shard_map.111 = (bf16[1,1,256,2560]{3,2,1,0:T(8,128)(2,1)}, bf16[1,128,512]{2,1,0:T(8,128)(2,1)}, bf16[1,128,512]{2,1,0:T(8,128)(2,1)}, f32[1,2560]{1,0:T(1,128)}, f32[1,512]{1,0:T(1,128)}) custom-call(bf16[1,1,256,2560]{3,2,1,0:T(8,128)(2,1)S(1)} %get-tuple-element.10.refs_0_, bf16[1,128,512]{2,1,0:T(8,128)(2,1)S(1)} %get-tuple-element.11.refs_1_, ...), custom_call_target="tpu_custom_call" | custom-call | tf_op jit(solution)/shard_map/pallas_call | solution.py:441

commit v3 on v2

--- a/solution.py
+++ b/solution.py
@@ -44,7 +44,8 @@
     (small_sem, q_sem, do_sem, kl_sem, vl_sem, kv_ss, kv_rs, g_ss, g_rs) = rest[n_st:n_st + 9]
     st_ss = rest[n_st + 9:2 * n_st + 9]
     st_rs = rest[2 * n_st + 9:3 * n_st + 9]
-    line_sems = rest[3 * n_st + 9:]
+    reply_sem = rest[3 * n_st + 9]
+    line_sems = rest[3 * n_st + 10:]
     groups, length, width = q_vm.shape
     per = width // HEAD
     rows = k_hbm.shape[1]
@@ -72,31 +73,37 @@
         return dp + (other - mine) * strides[s]
 
     near, far = near_split(stages)
-    row = dp // near if near else 0
+    row, seat = (dp // near, lax.rem(dp, near)) if near else (0, 0)
+
+    def dp_signal(sem, when, offset):
+        @pl.when(when)
+        def _():
+            pl.semaphore_signal(sem, inc=1, device_id={"dp": dp + offset}, device_id_type=MESH)
+
+    def signal_up(sem):
+        dp_signal(sem, row < far - 1, near)
+        for off in range(1, near):
+            dp_signal(sem, seat < near - off, off)
+
+    def signal_down(sem):
+        dp_signal(sem, row > 0, -near)
+        for off in range(1, near):
+            dp_signal(sem, seat >= off, -off)
 
     def line_signal(sem):
-        @pl.when(row > 0)
-        def _():
-            pl.semaphore_signal(sem, inc=1, device_id={"dp": dp - near}, device_id_type=MESH)
-
-        @pl.when(row < far - 1)
-        def _():
-            pl.semaphore_signal(sem, inc=1, device_id={"dp": dp + near}, device_id_type=MESH)
-
-    line_count = jnp.where(row > 0, 1, 0) + jnp.where(row < far - 1, 1, 0)
+        dp_signal(sem, row > 0, -near)
+        dp_signal(sem, row < far - 1, near)
+
+    below = jnp.where(row > 0, 1, 0)
+    above = jnp.where(row < far - 1, 1, 0)
     barrier = pltpu.get_barrier_semaphore()
     count = 0
     for off in range(1, sections):
         pl.semaphore_signal(barrier, inc=1, device_id={"section": sec_peer(off)}, device_id_type=MESH)
         count += 1
     if near:
-        for off in range(1, near):
-            other = row * near + lax.rem(lax.rem(dp, near) + off, near)
-            pl.semaphore_signal(barrier, inc=1, device_id={"dp": other}, device_id_type=MESH)
-            count += 1
-        if far > 1:
-            line_signal(barrier)
-            count = count + line_count
+        signal_up(barrier)
+        count = count + below + seat
     else:
         for s in range(n_st):
             for off in range(1, stages[s]):
@@ -161,9 +168,9 @@
 
     def st_total(s, g):
         drain(slots[s].at[g, :stages[s] - 1], st_rs[s].at[g])
-        total = slots[s][g, 0]
+        total = slots[s][g, 0].astype(F32)
         for m in range(1, stages[s]):
-            total = total + slots[s][g, m]
+            total = total + slots[s][g, m].astype(F32)
         return total
 
     def st_start(s, g):
@@ -171,7 +178,7 @@
             st_copy(s, g, off).start()
 
     def st_send(s, g, value):
-        slots[s][g, member(s)] = value
+        slots[s][g, member(s)] = value.astype(BF)
         st_start(s, g)
 
     small = [
@@ -189,14 +196,20 @@
 
     pl.semaphore_wait(barrier, count)
 
-    @pl.loop(0, groups)
-    def _(g):
-        for off in range(1, sections):
-            for c in kv_copies(g, off):
-                c.start()
-
-    if line_sems:
-        line_signal(line_sems[0])
+    def send_kv():
+        for g in range(groups):
+            for off in range(1, sections):
+                for c in kv_copies(g, off):
+                    c.start()
+
+    second = lax.rem(dp, 2) == 1
+
+    @pl.when(jnp.logical_not(second))
+    def _():
+        send_kv()
+
+    if near:
+        signal_down(reply_sem)
 
     for c in small:
         c.wait()
@@ -209,14 +222,32 @@
     bias[1] = shade[:half, half:]
     bias[2] = shade[half:, half:]
 
-    @pl.loop(0, groups)
-    def _(g):
+    def prepare(g):
         q_in(g).wait()
         for h in range(per):
             q_f = q_vm[g, :, h * HEAD:(h + 1) * HEAD].astype(F32)
             q_scale = qs_ref[:, pl.ds(pl.multiple_of(g * width + h * HEAD, HEAD), HEAD)]
             qf_vm[g, h] = q_f
             ql_vm[g, h] = (q_f * q_scale).astype(BF)
+
+    prepare(0)
+
+    @pl.when(second)
+    def _():
+        send_kv()
+
+    pl.loop(1, groups)(prepare)
+    if near:
+        replies = above + near - 1 - seat
+
+        @pl.when(replies > 0)
+        def _():
+            pl.semaphore_wait(reply_sem, replies)
+    for i, sem in enumerate(line_sems[:2]):
+        if i:
+            pl.semaphore_wait(line_sems[i - 1], below + above)
+        line_signal(sem)
+    early = len(line_sems[1:])
 
     def one_group(g, carry):
         for c in local_in(g):
@@ -316,14 +347,14 @@
         if spare:
             gain_rows.append(jnp.zeros((spare, HEAD), F32))
         gain_block = jnp.concatenate(gain_rows, axis=0)
-        slots[0][g, member(0)] = gain_block
-        for i in range(len(line_sems)):
+        slots[0][g, member(0)] = gain_block.astype(BF)
+        for i in range(early):
             @pl.when(g == i)
             def _():
-                pl.semaphore_wait(line_sems[i], line_count)
-                if i + 1 < len(line_sems):
-                    line_signal(line_sems[i + 1])
-        hold = max(len(line_sems) - 1, 0)
+                pl.semaphore_wait(line_sems[i + 1], below + above)
+                if i + 1 < early:
+                    line_signal(line_sems[i + 2])
+        hold = max(early - 1, 0)
 
         @pl.when(g == hold)
         def _():
@@ -418,11 +449,11 @@
             pltpu.VMEM((groups, length, 2 * HEAD), BF),
             pltpu.VMEM((peers, groups, rows, 2 * HEAD), BF),
         ]
-        scratch += [pltpu.VMEM((groups, r, gain_rows, HEAD), F32) for r in stages]
+        scratch += [pltpu.VMEM((groups, r, gain_rows, HEAD), BF) for r in stages]
         scratch += [dma((3,))] + [dma((groups,))] * 4
         scratch += [dma((peers,)), dma((peers, groups))] * 2
         scratch += [dma] * n_st + [dma((groups,))] * n_st
-        scratch += [pltpu.SemaphoreType.REGULAR] * max(near_split(stages)[1] - 1, 0)
+        scratch += [pltpu.SemaphoreType.REGULAR] * max(near_split(stages)[1], 1)
         shapes = (
             jax.ShapeDtypeStruct(queries.shape, BF),
             jax.ShapeDtypeStruct(keys.shape, BF),

time: 22.6 us -> 21.3 us (0.942)
  Pallas kernels: 21.1 us -> 19.8 us
    pallas_call x1, Pallas kernels: 20 us -> 18.7 us  [on_device(): pl.pallas_call(functools.partial(kernel, sections, replicas, stages), out...]
where the time goes in v3:
time: 21.3 us; the launch traced here: 21.1 us
  Pallas kernels  19.8 us (93%)
  between operations  1.29 us (6%)
    pallas_call x1, Pallas kernels, on_device(): pl.pallas_call(functools.partial(kernel, sections, replicas, stages), out...  18.7 us
    pallas_call x1, Pallas kernels, on_device(): pl.pallas_call(write_out, out_shape=shapes, in_specs=[vmem] * 5, out_spec...  1.18 us

profile of v3, /device:TPU:0, one launch (start us, length us, event | category | flops | bytes accessed | tf_op | source)
XLA Modules:
  0.0 21.1 jit_solution(399414754293928313)
XLA Ops:
  1.3 18.7 %shard_map.110 = (bf16[1,1,256,2560]{3,2,1,0:T(8,128)(2,1)S(1)}, bf16[1,128,512]{2,1,0:T(8,128)(2,1)S(1)}, bf16[1,128,512]{2,1,0:T(8,128)(2,1)S(1)}, f32[1,2560]{1,0:T(1,128)S(1)}, f32[1,512]{1,0:T(1,128)S(1)}) custom-call(s32[1]{0:T(128)S(6)} %copy.12.doc_hbm, bf16[1,1,256,2560]{3,2,1,0:T(8,128)(2,1)} %q_hbm.1, bf16[1,128,512]{2,1,0:T(8,128)(2,1)} %k_hbm.1, ...), custom_call_target="tpu_custom_call" | custom-call | tf_op jit(solution)/shard_map/pallas_call | solution.py:464
  20.0 1.2 %shard_map.111 = (bf16[1,1,256,2560]{3,2,1,0:T(8,128)(2,1)}, bf16[1,128,512]{2,1,0:T(8,128)(2,1)}, bf16[1,128,512]{2,1,0:T(8,128)(2,1)}, f32[1,2560]{1,0:T(1,128)}, f32[1,512]{1,0:T(1,128)}) custom-call(bf16[1,1,256,2560]{3,2,1,0:T(8,128)(2,1)S(1)} %get-tuple-element.10.refs_0_, bf16[1,128,512]{2,1,0:T(8,128)(2,1)S(1)} %get-tuple-element.11.refs_1_, ...), custom_call_target="tpu_custom_call" | custom-call | tf_op jit(solution)/shard_map/pallas_call | solution.py:472

commit v4 on v3

--- a/solution.py
+++ b/solution.py
@@ -41,11 +41,11 @@
 ):
     n_st = len(stages)
     slots = rest[:n_st]
-    (small_sem, q_sem, do_sem, kl_sem, vl_sem, kv_ss, kv_rs, g_ss, g_rs) = rest[n_st:n_st + 9]
-    st_ss = rest[n_st + 9:2 * n_st + 9]
-    st_rs = rest[2 * n_st + 9:3 * n_st + 9]
-    reply_sem = rest[3 * n_st + 9]
-    line_sems = rest[3 * n_st + 10:]
+    (small_sem, q_sem, do_sem, k_sem, v_sem, out_sem, g_rs) = rest[n_st:n_st + 7]
+    st_ss = rest[n_st + 7:2 * n_st + 7]
+    st_rs = rest[2 * n_st + 7:3 * n_st + 7]
+    reply_sem = rest[3 * n_st + 7]
+    line_sems = rest[3 * n_st + 8:]
     groups, length, width = q_vm.shape
     per = width // HEAD
     rows = k_hbm.shape[1]
@@ -120,22 +120,20 @@
 
     def local_in(g):
         return (
-            pltpu.make_async_copy(k_hbm.at[0, :, hcols(g)], k_vm.at[g, my_rows, :], kl_sem.at[g]),
-            pltpu.make_async_copy(v_hbm.at[0, :, hcols(g)], v_vm.at[g, my_rows, :], vl_sem.at[g]),
-            pltpu.make_async_copy(do_hbm.at[0, 0, :, wcols(g)], do_vm.at[g], do_sem.at[g]),
+            pltpu.make_async_copy(k_hbm.at[0, :, hcols(g)], k_vm.at[g, my_rows, :], k_sem.at[g]),
+            pltpu.make_async_copy(v_hbm.at[0, :, hcols(g)], v_vm.at[g, my_rows, :], v_sem.at[g]),
+            pltpu.make_async_copy(q_hbm.at[0, 0, :, wcols(g)], q_vm.at[g], q_sem),
+            pltpu.make_async_copy(do_hbm.at[0, 0, :, wcols(g)], do_vm.at[g], do_sem),
         )
-
-    def q_in(g):
-        return pltpu.make_async_copy(q_hbm.at[0, 0, :, wcols(g)], q_vm.at[g], q_sem.at[g])
 
     def kv_copies(g, off):
         made = []
-        for src, dst in ((k_hbm, k_vm), (v_hbm, v_vm)):
+        for src, dst, sem in ((k_hbm, k_vm, k_sem), (v_hbm, v_vm, v_sem)):
             made.append(pltpu.make_async_remote_copy(
                 src_ref=src.at[0, :, hcols(g)],
                 dst_ref=dst.at[g, my_rows, :],
-                send_sem=kv_ss.at[off - 1],
-                recv_sem=kv_rs.at[off - 1, g],
+                send_sem=out_sem.at[off - 1],
+                recv_sem=sem.at[g],
                 device_id={"section": sec_peer(off)},
                 device_id_type=MESH,
             ))
@@ -146,11 +144,14 @@
         return pltpu.make_async_remote_copy(
             src_ref=gsend.at[g, pl.ds(pl.multiple_of(peer * rows, rows), rows), :],
             dst_ref=grecv.at[off - 1, g],
-            send_sem=g_ss.at[off - 1],
-            recv_sem=g_rs.at[off - 1, g],
+            send_sem=out_sem.at[off - 1],
+            recv_sem=g_rs.at[off - 1],
             device_id={"section": peer},
             device_id_type=MESH,
         )
+
+    def arrival(g):
+        return g if n_st > 1 else jnp.where(g == groups - 1, 1, 0)
 
     def st_copy(s, g, off):
         mine = member(s)
@@ -158,7 +159,7 @@
             src_ref=slots[s].at[g, mine],
             dst_ref=slots[s].at[g, mine],
             send_sem=st_ss[s],
-            recv_sem=st_rs[s].at[g],
+            recv_sem=st_rs[s].at[arrival(g)],
             device_id={"dp": st_peer(s, off)},
             device_id_type=MESH,
         )
@@ -166,12 +167,15 @@
     def drain(ref, sem):
         pltpu.make_async_copy(ref, ref, sem).wait()
 
-    def st_total(s, g):
-        drain(slots[s].at[g, :stages[s] - 1], st_rs[s].at[g])
+    def slot_sum(s, g):
         total = slots[s][g, 0].astype(F32)
         for m in range(1, stages[s]):
             total = total + slots[s][g, m].astype(F32)
         return total
+
+    def st_total(s, g):
+        drain(slots[s].at[g, :stages[s] - 1], st_rs[s].at[g])
+        return slot_sum(s, g)
 
     def st_start(s, g):
         for off in range(1, stages[s]):
@@ -190,23 +194,23 @@
 
     @pl.loop(0, groups)
     def _(g):
-        q_in(g).start()
         for c in local_in(g):
             c.start()
 
     pl.semaphore_wait(barrier, count)
 
-    def send_kv():
-        for g in range(groups):
+    def send_kv(first, last):
+        for g in range(first, last):
             for off in range(1, sections):
                 for c in kv_copies(g, off):
                     c.start()
 
     second = lax.rem(dp, 2) == 1
+    send_kv(0, 1)
 
     @pl.when(jnp.logical_not(second))
     def _():
-        send_kv()
+        send_kv(1, groups)
 
     if near:
         signal_down(reply_sem)
@@ -222,45 +226,49 @@
     bias[1] = shade[:half, half:]
     bias[2] = shade[half:, half:]
 
+    drain(q_vm, q_sem)
+
     def prepare(g):
-        q_in(g).wait()
         for h in range(per):
             q_f = q_vm[g, :, h * HEAD:(h + 1) * HEAD].astype(F32)
             q_scale = qs_ref[:, pl.ds(pl.multiple_of(g * width + h * HEAD, HEAD), HEAD)]
             qf_vm[g, h] = q_f
             ql_vm[g, h] = (q_f * q_scale).astype(BF)
 
-    prepare(0)
+    pl.loop(0, groups)(prepare)
 
     @pl.when(second)
     def _():
-        send_kv()
-
-    pl.loop(1, groups)(prepare)
+        send_kv(1, groups)
+
     if near:
         replies = above + near - 1 - seat
 
         @pl.when(replies > 0)
         def _():
             pl.semaphore_wait(reply_sem, replies)
-    for i, sem in enumerate(line_sems[:2]):
-        if i:
-            pl.semaphore_wait(line_sems[i - 1], below + above)
-        line_signal(sem)
+    if line_sems:
+        line_signal(line_sems[0])
+
+    drain(do_vm, do_sem)
+    if line_sems:
+        pl.semaphore_wait(line_sems[0], below + above)
+    if line_sems[1:]:
+        line_signal(line_sems[1])
     early = len(line_sems[1:])
 
-    def one_group(g, carry):
-        for c in local_in(g):
-            c.wait()
-        for off in range(1, sections):
-            drain(grecv.at[off - 1, g], kv_rs.at[off - 1, g])
+    def when(cond):
+        if isinstance(cond, bool):
+            return lambda f: f() if cond else None
+        return pl.when(cond)
+
+    def one_group(g, last):
+        drain(k_vm.at[g], k_sem.at[g])
+        drain(v_vm.at[g], v_sem.at[g])
         k_scale = ks_ref[:, hcols(g)]
-        k_raw = k_vm[g].astype(F32)
-        k_low = (k_raw * k_scale).astype(BF)
+        k_low = (k_vm[g].astype(F32) * k_scale).astype(BF)
         k_t = k_low.astype(F32).T.astype(BF)
-        val = v_vm[g]
         k0, k1 = k_low[:half], k_low[half:]
-        v0, v1 = val[:half], val[half:]
         gain_rows = []
 
         def d_out_of(h):
@@ -274,9 +282,9 @@
 
         def d_probs(h):
             d_out = d_out_of(h)
-            x = lax.dot_general(v0, d_out, NT, preferred_element_type=F32)
+            x = lax.dot_general(v_vm[g, :half], d_out, NT, preferred_element_type=F32)
             dbuf[h % 2, 0], dbuf[h % 2, 1] = x[:, :half], x[:, half:]
-            dbuf[h % 2, 2] = lax.dot_general(v1, d_out[half:], NT, preferred_element_type=F32)
+            dbuf[h % 2, 2] = lax.dot_general(v_vm[g, half:], d_out[half:], NT, preferred_element_type=F32)
 
         def softmax(h, blocks):
             b = h % 2
@@ -289,11 +297,11 @@
             r = [p * dbuf[b, i] for p, i in zip(ps, blocks)]
             r = jnp.sum(functools.reduce(jnp.add, r), axis=0, keepdims=True)
             for p, i in zip(ps, blocks):
-                pbuf[b, i] = p.astype(BF)
-                dsbuf[b, i] = (p * (dbuf[b, i] - r)).astype(BF)
+                pbuf[h, i] = p.astype(BF)
+                dsbuf[h, i] = (p * (dbuf[b, i] - r)).astype(BF)
 
         def wide(ref, h):
-            return jnp.concatenate([ref[h % 2, 0], ref[h % 2, 1]], axis=1)
+            return jnp.concatenate([ref[h, 0], ref[h, 1]], axis=1)
 
         def add(h, rows_, cols_, x):
             if h == 0:
@@ -307,18 +315,62 @@
         def kv_grads(h):
             d_out, q_low = d_out_of(h), ql_vm[g, h]
             add(h, lo, vc, jnp.dot(wide(pbuf, h), d_out, preferred_element_type=F32))
-            add(h, hi, vc, jnp.dot(pbuf[h % 2, 2], d_out[half:], preferred_element_type=F32))
+            add(h, hi, vc, jnp.dot(pbuf[h, 2], d_out[half:], preferred_element_type=F32))
             add(h, lo, kc, jnp.dot(wide(dsbuf, h), q_low, preferred_element_type=F32))
-            add(h, hi, kc, jnp.dot(dsbuf[h % 2, 2], q_low[half:], preferred_element_type=F32))
+            add(h, hi, kc, jnp.dot(dsbuf[h, 2], q_low[half:], preferred_element_type=F32))
 
         def q_grads(h):
             ds_full = jnp.concatenate(
-                [wide(dsbuf, h), jnp.concatenate([jnp.zeros((half, half), BF), dsbuf[h % 2, 2]], axis=1)], axis=0
+                [wide(dsbuf, h), jnp.concatenate([jnp.zeros((half, half), BF), dsbuf[h, 2]], axis=1)], axis=0
             )
             cols = pl.ds(pl.multiple_of(g * width + h * HEAD, HEAD), HEAD)
             dq = jnp.dot(k_t, ds_full, preferred_element_type=F32).T
             dq_ref[0, 0, :, cols] = (dq * (qs_ref[:, cols] * scale)).astype(BF)
             gain_rows.append(jnp.sum(dq * qf_vm[g, h], axis=0, keepdims=True))
+
+        def all_kv_grads():
+            heads = range(per)
+            for ref, right, cols in (
+                (pbuf, [d_out_of(h) for h in heads], vc),
+                (dsbuf, [ql_vm[g, h] for h in heads], kc),
+            ):
+                grad[g, lo, cols] = jnp.dot(
+                    jnp.concatenate([wide(ref, h) for h in heads], axis=1),
+                    jnp.concatenate(right, axis=0), preferred_element_type=F32,
+                )
+                grad[g, hi, cols] = jnp.dot(
+                    jnp.concatenate([ref[h, 2] for h in heads], axis=1),
+                    jnp.concatenate([x[half:] for x in right], axis=0), preferred_element_type=F32,
+                )
+
+        def send_grads():
+            key_term = grad[g, :, kc] * (k_scale * scale)
+            grad[g, :, kc] = key_term
+            gsend[g, :, kc] = key_term.astype(BF)
+            gsend[g, :, vc] = grad[g, :, vc].astype(BF)
+            for off in range(1, sections):
+                grad_copy(g, off).start()
+
+        def send_gains():
+            spare = slots[0].shape[2] - per
+            rows_ = gain_rows + ([jnp.zeros((spare, HEAD), F32)] if spare else [])
+            slots[0][g, member(0)] = jnp.concatenate(rows_, axis=0).astype(BF)
+            for i in range(early):
+                @when(g == i)
+                def _():
+                    pl.semaphore_wait(line_sems[i + 1], below + above)
+                    if i + 1 < early:
+                        line_signal(line_sems[i + 2])
+            hold = max(early - 1, 0)
+
+            @when(g == hold)
+            def _():
+                for e in range(hold):
+                    st_start(0, e)
+
+            @when(g >= hold)
+            def _():
+                st_start(0, g)
 
         scores(0)
         d_probs(0)
@@ -328,61 +380,43 @@
             softmax(h, (0,))
             if h + 1 < per:
                 d_probs(h + 1)
-            if h:
+            if h and not last:
                 kv_grads(h - 1)
             softmax(h, (1, 2))
             if h:
                 q_grads(h - 1)
-        kv_grads(per - 1)
-        q_grads(per - 1)
-        dk = grad[g, :, :HEAD]
-        key_term = dk * (k_scale * scale)
-        grad[g, :, :HEAD] = key_term
-        gsend[g, :, :HEAD] = key_term.astype(BF)
-        gsend[g, :, HEAD:] = grad[g, :, HEAD:].astype(BF)
-        for off in range(1, sections):
-            grad_copy(g, off).start()
-        gain_rows.append(jnp.sum(dk * k_raw, axis=0, keepdims=True))
-        spare = slots[0].shape[2] - len(gain_rows)
-        if spare:
-            gain_rows.append(jnp.zeros((spare, HEAD), F32))
-        gain_block = jnp.concatenate(gain_rows, axis=0)
-        slots[0][g, member(0)] = gain_block.astype(BF)
-        for i in range(early):
-            @pl.when(g == i)
-            def _():
-                pl.semaphore_wait(line_sems[i + 1], below + above)
-                if i + 1 < early:
-                    line_signal(line_sems[i + 2])
-        hold = max(early - 1, 0)
-
-        @pl.when(g == hold)
-        def _():
-            for e in range(hold):
-                st_start(0, e)
-
-        @pl.when(g >= hold)
-        def _():
-            st_start(0, g)
+        if last:
+            q_grads(per - 1)
+            send_gains()
+            all_kv_grads()
+            send_grads()
+        else:
+            kv_grads(per - 1)
+            q_grads(per - 1)
+            send_grads()
+            send_gains()
 
         for s in range(1, n_st):
-            @pl.when(g >= LAG * s)
+            @when(g >= LAG * s)
             def _():
                 st_send(s, g - LAG * s, st_total(s - 1, g - LAG * s))
-        return carry
-
-    lax.fori_loop(0, groups, one_group, 0)
-
-    def finish_gain(g):
-        total = st_total(n_st - 1, g) * (scale / replicas)
+
+    pl.loop(0, groups - 1)(lambda g: one_group(g, False))
+    one_group(groups - 1, True)
+
+    def finish_gain(g, total):
+        total = total * (scale / replicas)
+        key_sum = 0.0
         for h in range(per):
-            qgain_ref[:, (g * per + h) * HEAD:(g * per + h + 1) * HEAD] = total[h:h + 1]
-        kgain_ref[:, g * HEAD:(g + 1) * HEAD] = total[per:per + 1]
+            cols = slice((g * per + h) * HEAD, (g * per + h + 1) * HEAD)
+            qgain_ref[:, cols] = total[h:h + 1]
+            key_sum = key_sum + total[h:h + 1] * qs_ref[:, cols]
+        cols = slice(g * HEAD, (g + 1) * HEAD)
+        kgain_ref[:, cols] = key_sum / ks_ref[:, cols]
 
     def finish_grad(g):
         total = grad[g, my_rows, :]
         for off in range(1, sections):
-            grad_copy(g, off).wait_recv()
             total = total + grecv[off - 1, g].astype(F32)
         kg_ref[0, :, g * HEAD:(g + 1) * HEAD] = total[:, :HEAD].astype(BF)
         vg_ref[0, :, g * HEAD:(g + 1) * HEAD] = total[:, HEAD:].astype(BF)
@@ -392,14 +426,23 @@
             g = t - LAG * s
             if 0 <= g < groups:
                 st_send(s, g, st_total(s - 1, g))
+    if n_st == 1 and groups > 1:
+        drain(slots[0].at[:groups - 1, :stages[0] - 1], st_rs[0].at[0])
+        for g in range(groups - 1):
+            finish_gain(g, slot_sum(0, g))
+    for off in range(1, sections):
+        drain(grecv.at[off - 1], g_rs.at[off - 1])
     for g in range(groups):
         finish_grad(g)
-    for g in range(groups):
-        finish_gain(g)
-
     for off in range(1, sections):
-        drain(grecv.at[off - 1], kv_ss.at[off - 1])
-        drain(grecv.at[off - 1], g_ss.at[off - 1])
+        drain(gsend.at[:, :2 * rows], out_sem.at[off - 1])
+    if n_st == 1:
+        drain(slots[0].at[0, :stages[0] - 1], st_rs[0].at[1])
+        finish_gain(groups - 1, slot_sum(0, groups - 1))
+    else:
+        for g in range(groups):
+            finish_gain(g, st_total(n_st - 1, g))
+
     for s in range(n_st):
         drain(slots[s].at[:, :stages[s] - 1], st_ss[s])
 
@@ -425,7 +468,8 @@
         rows, kv_width = keys.shape[1], keys.shape[2]
         groups, half = kv_width // HEAD, length // 2
         width = queries.shape[3] // groups
-        gain_rows = -(-(width // HEAD + 1) // 8) * 8
+        per = width // HEAD
+        gain_rows = -(-per // 8) * 8
         vmem = pl.BlockSpec(memory_space=pltpu.VMEM)
         hbm = pl.BlockSpec(memory_space=pl.ANY)
         dma = pltpu.SemaphoreType.DMA
@@ -442,17 +486,16 @@
             pltpu.VMEM((groups, width // HEAD, length, HEAD), F32),
             pltpu.VMEM((2, 3, half, half), F32),
             pltpu.VMEM((2, 3, half, half), F32),
-            pltpu.VMEM((2, 3, half, half), BF),
-            pltpu.VMEM((2, 3, half, half), BF),
+            pltpu.VMEM((per, 3, half, half), BF),
+            pltpu.VMEM((per, 3, half, half), BF),
             pltpu.VMEM((3, half, half), F32),
             pltpu.VMEM((groups, length, 2 * HEAD), F32),
             pltpu.VMEM((groups, length, 2 * HEAD), BF),
             pltpu.VMEM((peers, groups, rows, 2 * HEAD), BF),
         ]
         scratch += [pltpu.VMEM((groups, r, gain_rows, HEAD), BF) for r in stages]
-        scratch += [dma((3,))] + [dma((groups,))] * 4
-        scratch += [dma((peers,)), dma((peers, groups))] * 2
-        scratch += [dma] * n_st + [dma((groups,))] * n_st
+        scratch += [dma((3,)), dma, dma, dma((groups,)), dma((groups,)), dma((peers,)), dma((peers,))]
+        scratch += [dma] * n_st + [dma((groups if n_st > 1 else 2,))] * n_st
         scratch += [pltpu.SemaphoreType.REGULAR] * max(near_split(stages)[1], 1)
         shapes = (
             jax.ShapeDtypeStruct(queries.shape, BF),

time: 21.3 us -> 20.7 us (0.972)
  Pallas kernels: 19.8 us -> 19.3 us
    pallas_call x1, Pallas kernels: 18.7 us -> 18.1 us  [on_device(): pl.pallas_call(functools.partial(kernel, sections, replicas, stages), out...]
where the time goes in v4:
time: 20.7 us; the launch traced here: 20.6 us
  Pallas kernels  19.3 us (93%)
  between operations  1.29 us (6%)
    pallas_call x1, Pallas kernels, on_device(): pl.pallas_call(functools.partial(kernel, sections, replicas, stages), out...  18.1 us
    pallas_call x1, Pallas kernels, on_device(): pl.pallas_call(write_out, out_shape=shapes, in_specs=[vmem] * 5, out_spec...  1.18 us

profile of v4, /device:TPU:0, one launch (start us, length us, event | category | flops | bytes accessed | tf_op | source)
XLA Modules:
  0.0 20.6 jit_solution(8420377633865910883)
XLA Ops:
  1.3 18.1 %shard_map.110 = (bf16[1,1,256,2560]{3,2,1,0:T(8,128)(2,1)S(1)}, bf16[1,128,512]{2,1,0:T(8,128)(2,1)S(1)}, bf16[1,128,512]{2,1,0:T(8,128)(2,1)S(1)}, f32[1,2560]{1,0:T(1,128)S(1)}, f32[1,512]{1,0:T(1,128)S(1)}) custom-call(s32[1]{0:T(128)S(6)} %copy.12.doc_hbm, bf16[1,1,256,2560]{3,2,1,0:T(8,128)(2,1)} %q_hbm.1, bf16[1,128,512]{2,1,0:T(8,128)(2,1)} %k_hbm.1, ...), custom_call_target="tpu_custom_call" | custom-call | tf_op jit(solution)/shard_map/pallas_call | solution.py:507
  19.4 1.2 %shard_map.111 = (bf16[1,1,256,2560]{3,2,1,0:T(8,128)(2,1)}, bf16[1,128,512]{2,1,0:T(8,128)(2,1)}, bf16[1,128,512]{2,1,0:T(8,128)(2,1)}, f32[1,2560]{1,0:T(1,128)}, f32[1,512]{1,0:T(1,128)}) custom-call(bf16[1,1,256,2560]{3,2,1,0:T(8,128)(2,1)S(1)} %get-tuple-element.10.refs_0_, bf16[1,128,512]{2,1,0:T(8,128)(2,1)S(1)} %get-tuple-element.11.refs_1_, ...), custom_call_target="tpu_custom_call" | custom-call | tf_op jit(solution)/shard_map/pallas_call | solution.py:515

commit v5 on v4

--- a/solution.py
+++ b/solution.py
@@ -37,11 +37,11 @@
     sections, replicas, stages,
     doc_hbm, q_hbm, k_hbm, v_hbm, qs_hbm, ks_hbm, do_hbm,
     dq_ref, kg_ref, vg_ref, qgain_ref, kgain_ref,
-    doc_ref, qs_ref, ks_ref, q_vm, do_vm, k_vm, v_vm, ql_vm, qf_vm, sbuf, dbuf, pbuf, dsbuf, bias, grad, gsend, grecv, *rest,
+    doc_ref, qs_ref, ks_ref, q_vm, do_vm, k_vm, v_vm, ql_vm, qf_vm, sbuf, dbuf, pbuf, dsbuf, plo, dslo, bias, grad, gsend, grecv, *rest,
 ):
     n_st = len(stages)
     slots = rest[:n_st]
-    (small_sem, q_sem, do_sem, k_sem, v_sem, out_sem, g_rs) = rest[n_st:n_st + 7]
+    (small_sem, q_sem, do_sem, own_sem, kv_sem, out_sem, g_rs) = rest[n_st:n_st + 7]
     st_ss = rest[n_st + 7:2 * n_st + 7]
     st_rs = rest[2 * n_st + 7:3 * n_st + 7]
     reply_sem = rest[3 * n_st + 7]
@@ -120,20 +120,20 @@
 
     def local_in(g):
         return (
-            pltpu.make_async_copy(k_hbm.at[0, :, hcols(g)], k_vm.at[g, my_rows, :], k_sem.at[g]),
-            pltpu.make_async_copy(v_hbm.at[0, :, hcols(g)], v_vm.at[g, my_rows, :], v_sem.at[g]),
+            pltpu.make_async_copy(k_hbm.at[0, :, hcols(g)], k_vm.at[g, my_rows, :], own_sem),
+            pltpu.make_async_copy(v_hbm.at[0, :, hcols(g)], v_vm.at[g, my_rows, :], own_sem),
             pltpu.make_async_copy(q_hbm.at[0, 0, :, wcols(g)], q_vm.at[g], q_sem),
             pltpu.make_async_copy(do_hbm.at[0, 0, :, wcols(g)], do_vm.at[g], do_sem),
         )
 
     def kv_copies(g, off):
         made = []
-        for src, dst, sem in ((k_hbm, k_vm, k_sem), (v_hbm, v_vm, v_sem)):
+        for src, dst in ((k_hbm, k_vm), (v_hbm, v_vm)):
             made.append(pltpu.make_async_remote_copy(
                 src_ref=src.at[0, :, hcols(g)],
                 dst_ref=dst.at[g, my_rows, :],
                 send_sem=out_sem.at[off - 1],
-                recv_sem=sem.at[g],
+                recv_sem=kv_sem.at[g],
                 device_id={"section": sec_peer(off)},
                 device_id_type=MESH,
             ))
@@ -251,6 +251,38 @@
         line_signal(line_sems[0])
 
     drain(do_vm, do_sem)
+    drain(grecv.at[0], own_sem)
+
+    def weigh(xs, ds):
+        top = jnp.max(functools.reduce(jnp.maximum, xs), axis=0, keepdims=True)
+        es = [jnp.exp2((x - top) * to_exp2) for x in xs]
+        inv = 1.0 / jnp.sum(functools.reduce(jnp.add, es), axis=0, keepdims=True)
+        ps = [e * inv for e in es]
+        r = [p * d[...] for p, d in zip(ps, ds)]
+        r = jnp.sum(functools.reduce(jnp.add, r), axis=0, keepdims=True)
+        return [(p.astype(BF), (p * (d[...] - r)).astype(BF)) for p, d in zip(ps, ds)]
+
+    lead = rows >= half
+
+    def ahead(g):
+        k_low = (k_vm[g, :half].astype(F32) * ks_ref[:, hcols(g)]).astype(BF)
+
+        def dots(h):
+            d_out = do_vm[g, :half, h * HEAD:(h + 1) * HEAD]
+            sbuf[h % 2, 0] = lax.dot_general(k_low, ql_vm[g, h, :half], NT, preferred_element_type=F32)
+            dbuf[h % 2, 0] = lax.dot_general(v_vm[g, :half], d_out, NT, preferred_element_type=F32)
+
+        dots(0)
+        for h in range(per):
+            if h + 1 < per:
+                dots(h + 1)
+            plo[g, h], dslo[g, h] = weigh([sbuf[h % 2, 0] + bias[0]], [dbuf.at[h % 2, 0]])[0]
+
+    if lead:
+        @pl.when(sec == 0)
+        def _():
+            pl.loop(0, groups)(ahead)
+
     if line_sems:
         pl.semaphore_wait(line_sems[0], below + above)
     if line_sems[1:]:
@@ -262,12 +294,10 @@
             return lambda f: f() if cond else None
         return pl.when(cond)
 
-    def one_group(g, last):
-        drain(k_vm.at[g], k_sem.at[g])
-        drain(v_vm.at[g], v_sem.at[g])
+    def one_group(g, last, early_lo):
+        drain(grecv.at[:, g], kv_sem.at[g])
         k_scale = ks_ref[:, hcols(g)]
         k_low = (k_vm[g].astype(F32) * k_scale).astype(BF)
-        k_t = k_low.astype(F32).T.astype(BF)
         k0, k1 = k_low[:half], k_low[half:]
         gain_rows = []
 
@@ -276,32 +306,34 @@
 
         def scores(h):
             q_low = ql_vm[g, h]
-            x = lax.dot_general(k0, q_low, NT, preferred_element_type=F32)
-            sbuf[h % 2, 0], sbuf[h % 2, 1] = x[:, :half], x[:, half:]
+            if early_lo:
+                sbuf[h % 2, 1] = lax.dot_general(k0, q_low[half:], NT, preferred_element_type=F32)
+            else:
+                x = lax.dot_general(k0, q_low, NT, preferred_element_type=F32)
+                sbuf[h % 2, 0], sbuf[h % 2, 1] = x[:, :half], x[:, half:]
             sbuf[h % 2, 2] = lax.dot_general(k1, q_low[half:], NT, preferred_element_type=F32)
 
         def d_probs(h):
             d_out = d_out_of(h)
-            x = lax.dot_general(v_vm[g, :half], d_out, NT, preferred_element_type=F32)
-            dbuf[h % 2, 0], dbuf[h % 2, 1] = x[:, :half], x[:, half:]
+            if early_lo:
+                dbuf[h % 2, 1] = lax.dot_general(v_vm[g, :half], d_out[half:], NT, preferred_element_type=F32)
+            else:
+                x = lax.dot_general(v_vm[g, :half], d_out, NT, preferred_element_type=F32)
+                dbuf[h % 2, 0], dbuf[h % 2, 1] = x[:, :half], x[:, half:]
             dbuf[h % 2, 2] = lax.dot_general(v_vm[g, half:], d_out[half:], NT, preferred_element_type=F32)
 
         def softmax(h, blocks):
             b = h % 2
-            xs = [sbuf[b, i] + bias[i] for i in blocks]
-            top = functools.reduce(jnp.maximum, xs)
-            top = jnp.max(top, axis=0, keepdims=True)
-            es = [jnp.exp2((x - top) * to_exp2) for x in xs]
-            inv = 1.0 / jnp.sum(functools.reduce(jnp.add, es), axis=0, keepdims=True)
-            ps = [e * inv for e in es]
-            r = [p * dbuf[b, i] for p, i in zip(ps, blocks)]
-            r = jnp.sum(functools.reduce(jnp.add, r), axis=0, keepdims=True)
-            for p, i in zip(ps, blocks):
-                pbuf[h, i] = p.astype(BF)
-                dsbuf[h, i] = (p * (dbuf[b, i] - r)).astype(BF)
+            made = weigh([sbuf[b, i] + bias[i] for i in blocks], [dbuf.at[b, i] for i in blocks])
+            for i, (p, ds) in zip(blocks, made):
+                if i:
+                    pbuf[h, i - 1], dsbuf[h, i - 1] = p, ds
+                else:
+                    plo[g, h], dslo[g, h] = p, ds
 
         def wide(ref, h):
-            return jnp.concatenate([ref[h, 0], ref[h, 1]], axis=1)
+            first = plo if ref is pbuf else dslo
+            return jnp.concatenate([first[g, h], ref[h, 0]], axis=1)
 
         def add(h, rows_, cols_, x):
             if h == 0:
@@ -315,16 +347,17 @@
         def kv_grads(h):
             d_out, q_low = d_out_of(h), ql_vm[g, h]
             add(h, lo, vc, jnp.dot(wide(pbuf, h), d_out, preferred_element_type=F32))
-            add(h, hi, vc, jnp.dot(pbuf[h, 2], d_out[half:], preferred_element_type=F32))
+            add(h, hi, vc, jnp.dot(pbuf[h, 1], d_out[half:], preferred_element_type=F32))
             add(h, lo, kc, jnp.dot(wide(dsbuf, h), q_low, preferred_element_type=F32))
-            add(h, hi, kc, jnp.dot(dsbuf[h, 2], q_low[half:], preferred_element_type=F32))
+            add(h, hi, kc, jnp.dot(dsbuf[h, 1], q_low[half:], preferred_element_type=F32))
 
         def q_grads(h):
-            ds_full = jnp.concatenate(
-                [wide(dsbuf, h), jnp.concatenate([jnp.zeros((half, half), BF), dsbuf[h, 2]], axis=1)], axis=0
-            )
             cols = pl.ds(pl.multiple_of(g * width + h * HEAD, HEAD), HEAD)
-            dq = jnp.dot(k_t, ds_full, preferred_element_type=F32).T
+            hi_ds = jnp.concatenate([dsbuf[h, 0], dsbuf[h, 1]], axis=0)
+            dq = jnp.concatenate([
+                lax.dot_general(dslo[g, h], k_low[:half], (((0,), (0,)), ((), ())), preferred_element_type=F32),
+                lax.dot_general(hi_ds, k_low, (((0,), (0,)), ((), ())), preferred_element_type=F32),
+            ], axis=0)
             dq_ref[0, 0, :, cols] = (dq * (qs_ref[:, cols] * scale)).astype(BF)
             gain_rows.append(jnp.sum(dq * qf_vm[g, h], axis=0, keepdims=True))
 
@@ -339,7 +372,7 @@
                     jnp.concatenate(right, axis=0), preferred_element_type=F32,
                 )
                 grad[g, hi, cols] = jnp.dot(
-                    jnp.concatenate([ref[h, 2] for h in heads], axis=1),
+                    jnp.concatenate([ref[h, 1] for h in heads], axis=1),
                     jnp.concatenate([x[half:] for x in right], axis=0), preferred_element_type=F32,
                 )
 
@@ -377,13 +410,16 @@
         for h in range(per):
             if h + 1 < per:
                 scores(h + 1)
-            softmax(h, (0,))
+            if not early_lo:
+                softmax(h, (0,))
             if h + 1 < per:
                 d_probs(h + 1)
             if h and not last:
                 kv_grads(h - 1)
             softmax(h, (1, 2))
-            if h:
+            if h > 1 and not last:
+                q_grads(h - 2)
+            if h and last:
                 q_grads(h - 1)
         if last:
             q_grads(per - 1)
@@ -391,6 +427,8 @@
             all_kv_grads()
             send_grads()
         else:
+            if per > 1:
+                q_grads(per - 2)
             kv_grads(per - 1)
             q_grads(per - 1)
             send_grads()
@@ -401,8 +439,20 @@
             def _():
                 st_send(s, g - LAG * s, st_total(s - 1, g - LAG * s))
 
-    pl.loop(0, groups - 1)(lambda g: one_group(g, False))
-    one_group(groups - 1, True)
+    def all_groups(early_lo):
+        pl.loop(0, groups - 1)(lambda g: one_group(g, False, early_lo))
+        one_group(groups - 1, True, early_lo)
+
+    if lead:
+        @pl.when(sec == 0)
+        def _():
+            all_groups(True)
+
+        @pl.when(sec != 0)
+        def _():
+            all_groups(False)
+    else:
+        all_groups(False)
 
     def finish_gain(g, total):
         total = total * (scale / replicas)
@@ -486,15 +536,17 @@
             pltpu.VMEM((groups, width // HEAD, length, HEAD), F32),
             pltpu.VMEM((2, 3, half, half), F32),
             pltpu.VMEM((2, 3, half, half), F32),
-            pltpu.VMEM((per, 3, half, half), BF),
-            pltpu.VMEM((per, 3, half, half), BF),
+            pltpu.VMEM((per, 2, half, half), BF),
+            pltpu.VMEM((per, 2, half, half), BF),
+            pltpu.VMEM((groups, per, half, half), BF),
+            pltpu.VMEM((groups, per, half, half), BF),
             pltpu.VMEM((3, half, half), F32),
             pltpu.VMEM((groups, length, 2 * HEAD), F32),
             pltpu.VMEM((groups, length, 2 * HEAD), BF),
             pltpu.VMEM((peers, groups, rows, 2 * HEAD), BF),
         ]
         scratch += [pltpu.VMEM((groups, r, gain_rows, HEAD), BF) for r in stages]
-        scratch += [dma((3,)), dma, dma, dma((groups,)), dma((groups,)), dma((peers,)), dma((peers,))]
+        scratch += [dma((3,)), dma, dma, dma, dma((groups,)), dma((peers,)), dma((peers,))]
         scratch += [dma] * n_st + [dma((groups if n_st > 1 else 2,))] * n_st
         scratch += [pltpu.SemaphoreType.REGULAR] * max(near_split(stages)[1], 1)
         shapes = (

time: 20.7 us -> 20.6 us (level)
  no operation moved by 1% of the time
where the time goes in v5:
time: 20.6 us; the launch traced here: 20.4 us
  Pallas kernels  19.1 us (93%)
  between operations  1.29 us (6%)
    pallas_call x1, Pallas kernels, on_device(): pl.pallas_call(functools.partial(kernel, sections, replicas, stages), out...  17.9 us
    pallas_call x1, Pallas kernels, on_device(): pl.pallas_call(write_out, out_shape=shapes, in_specs=[vmem] * 5, out_spec...  1.18 us

profile of v5, /device:TPU:0, one launch (start us, length us, event | category | flops | bytes accessed | tf_op | source)
XLA Modules:
  0.0 20.4 jit_solution(3806426316460559605)
XLA Ops:
  1.3 17.9 %shard_map.110 = (bf16[1,1,256,2560]{3,2,1,0:T(8,128)(2,1)S(1)}, bf16[1,128,512]{2,1,0:T(8,128)(2,1)S(1)}, bf16[1,128,512]{2,1,0:T(8,128)(2,1)S(1)}, f32[1,2560]{1,0:T(1,128)S(1)}, f32[1,512]{1,0:T(1,128)S(1)}) custom-call(s32[1]{0:T(128)S(6)} %copy.12.doc_hbm, bf16[1,1,256,2560]{3,2,1,0:T(8,128)(2,1)} %q_hbm.1, bf16[1,128,512]{2,1,0:T(8,128)(2,1)} %k_hbm.1, ...), custom_call_target="tpu_custom_call" | custom-call | tf_op jit(solution)/shard_map/pallas_call | solution.py:559
  19.2 1.2 %shard_map.111 = (bf16[1,1,256,2560]{3,2,1,0:T(8,128)(2,1)}, bf16[1,128,512]{2,1,0:T(8,128)(2,1)}, bf16[1,128,512]{2,1,0:T(8,128)(2,1)}, f32[1,2560]{1,0:T(1,128)}, f32[1,512]{1,0:T(1,128)}) custom-call(bf16[1,1,256,2560]{3,2,1,0:T(8,128)(2,1)S(1)} %get-tuple-element.10.refs_0_, bf16[1,128,512]{2,1,0:T(8,128)(2,1)S(1)} %get-tuple-element.11.refs_1_, ...), custom_call_target="tpu_custom_call" | custom-call | tf_op jit(solution)/shard_map/pallas_call | solution.py:567

commit v6 on v5

--- a/solution.py
+++ b/solution.py
@@ -376,13 +376,23 @@
                     jnp.concatenate([x[half:] for x in right], axis=0), preferred_element_type=F32,
                 )
 
+        def start_grad(e):
+            for off in range(1, sections):
+                grad_copy(e, off).start()
+
         def send_grads():
             key_term = grad[g, :, kc] * (k_scale * scale)
             grad[g, :, kc] = key_term
             gsend[g, :, kc] = key_term.astype(BF)
             gsend[g, :, vc] = grad[g, :, vc].astype(BF)
-            for off in range(1, sections):
-                grad_copy(g, off).start()
+            if last:
+                start_grad(g)
+                return
+
+            @when(g == groups - 2)
+            def _():
+                for e in range(groups - 1):
+                    start_grad(e)
 
         def send_gains():
             spare = slots[0].shape[2] - per

time: 20.6 us -> 20.4 us (level)
  no operation moved by 1% of the time
where the time goes in v6:
time: 20.4 us; the launch traced here: 20.2 us
  Pallas kernels  18.9 us (93%)
  between operations  1.29 us (6%)
    pallas_call x1, Pallas kernels, on_device(): pl.pallas_call(functools.partial(kernel, sections, replicas, stages), out...  17.7 us
    pallas_call x1, Pallas kernels, on_device(): pl.pallas_call(write_out, out_shape=shapes, in_specs=[vmem] * 5, out_spec...  1.18 us

profile of v6, /device:TPU:0, one launch (start us, length us, event | category | flops | bytes accessed | tf_op | source)
XLA Modules:
  0.0 20.2 jit_solution(3009541714026872688)
XLA Ops:
  1.3 17.7 %shard_map.110 = (bf16[1,1,256,2560]{3,2,1,0:T(8,128)(2,1)S(1)}, bf16[1,128,512]{2,1,0:T(8,128)(2,1)S(1)}, bf16[1,128,512]{2,1,0:T(8,128)(2,1)S(1)}, f32[1,2560]{1,0:T(1,128)S(1)}, f32[1,512]{1,0:T(1,128)S(1)}) custom-call(s32[1]{0:T(128)S(6)} %copy.12.doc_hbm, bf16[1,1,256,2560]{3,2,1,0:T(8,128)(2,1)} %q_hbm.1, bf16[1,128,512]{2,1,0:T(8,128)(2,1)} %k_hbm.1, ...), custom_call_target="tpu_custom_call" | custom-call | tf_op jit(solution)/shard_map/pallas_call | solution.py:569
  19.0 1.2 %shard_map.111 = (bf16[1,1,256,2560]{3,2,1,0:T(8,128)(2,1)}, bf16[1,128,512]{2,1,0:T(8,128)(2,1)}, bf16[1,128,512]{2,1,0:T(8,128)(2,1)}, f32[1,2560]{1,0:T(1,128)}, f32[1,512]{1,0:T(1,128)}) custom-call(bf16[1,1,256,2560]{3,2,1,0:T(8,128)(2,1)S(1)} %get-tuple-element.10.refs_0_, bf16[1,128,512]{2,1,0:T(8,128)(2,1)S(1)} %get-tuple-element.11.refs_1_, ...), custom_call_target="tpu_custom_call" | custom-call | tf_op jit(solution)/shard_map/pallas_call | solution.py:577

commit v7 on v6

--- a/solution.py
+++ b/solution.py
@@ -241,15 +241,6 @@
     def _():
         send_kv(1, groups)
 
-    if near:
-        replies = above + near - 1 - seat
-
-        @pl.when(replies > 0)
-        def _():
-            pl.semaphore_wait(reply_sem, replies)
-    if line_sems:
-        line_signal(line_sems[0])
-
     drain(do_vm, do_sem)
     drain(grecv.at[0], own_sem)
 
@@ -281,7 +272,21 @@
     if lead:
         @pl.when(sec == 0)
         def _():
-            pl.loop(0, groups)(ahead)
+            pl.loop(0, groups // 2)(ahead)
+
+    if near:
+        replies = above + near - 1 - seat
+
+        @pl.when(replies > 0)
+        def _():
+            pl.semaphore_wait(reply_sem, replies)
+    if line_sems:
+        line_signal(line_sems[0])
+
+    if lead:
+        @pl.when(sec == 0)
+        def _():
+            pl.loop(groups // 2, groups)(ahead)
 
     if line_sems:
         pl.semaphore_wait(line_sems[0], below + above)
@@ -424,17 +429,18 @@
                 softmax(h, (0,))
             if h + 1 < per:
                 d_probs(h + 1)
-            if h and not last:
-                kv_grads(h - 1)
+            if h > 1 or (h and not last):
+                kv_grads(h - 1 - int(last))
             softmax(h, (1, 2))
-            if h > 1 and not last:
+            if h > 1:
                 q_grads(h - 2)
-            if h and last:
-                q_grads(h - 1)
         if last:
+            if per > 1:
+                q_grads(per - 2)
             q_grads(per - 1)
             send_gains()
-            all_kv_grads()
+            kv_grads(per - 2)
+            kv_grads(per - 1)
             send_grads()
         else:
             if per > 1:

time: 20.4 us -> 20.4 us (level)
  no operation moved by 1% of the time
where the time goes in v7:
time: 20.4 us; the launch traced here: 20.2 us
  Pallas kernels  18.9 us (93%)
  between operations  1.29 us (6%)
    pallas_call x1, Pallas kernels, on_device(): pl.pallas_call(functools.partial(kernel, sections, replicas, stages), out...  17.7 us
    pallas_call x1, Pallas kernels, on_device(): pl.pallas_call(write_out, out_shape=shapes, in_specs=[vmem] * 5, out_spec...  1.18 us

profile of v7, /device:TPU:0, one launch (start us, length us, event | category | flops | bytes accessed | tf_op | source)
XLA Modules:
  0.0 20.2 jit_solution(7836889467296222846)
XLA Ops:
  1.3 17.7 %shard_map.110 = (bf16[1,1,256,2560]{3,2,1,0:T(8,128)(2,1)S(1)}, bf16[1,128,512]{2,1,0:T(8,128)(2,1)S(1)}, bf16[1,128,512]{2,1,0:T(8,128)(2,1)S(1)}, f32[1,2560]{1,0:T(1,128)S(1)}, f32[1,512]{1,0:T(1,128)S(1)}) custom-call(s32[1]{0:T(128)S(6)} %copy.12.doc_hbm, bf16[1,1,256,2560]{3,2,1,0:T(8,128)(2,1)} %q_hbm.1, bf16[1,128,512]{2,1,0:T(8,128)(2,1)} %k_hbm.1, ...), custom_call_target="tpu_custom_call" | custom-call | tf_op jit(solution)/shard_map/pallas_call | solution.py:575
  19.0 1.2 %shard_map.111 = (bf16[1,1,256,2560]{3,2,1,0:T(8,128)(2,1)}, bf16[1,128,512]{2,1,0:T(8,128)(2,1)}, bf16[1,128,512]{2,1,0:T(8,128)(2,1)}, f32[1,2560]{1,0:T(1,128)}, f32[1,512]{1,0:T(1,128)}) custom-call(bf16[1,1,256,2560]{3,2,1,0:T(8,128)(2,1)S(1)} %get-tuple-element.10.refs_0_, bf16[1,128,512]{2,1,0:T(8,128)(2,1)S(1)} %get-tuple-element.11.refs_1_, ...), custom_call_target="tpu_custom_call" | custom-call | tf_op jit(solution)/shard_map/pallas_call | solution.py:583
